TPU v7x, 32 devices: a whole 2x2x4 slice. The times are simulated.
32 devices in a mesh: dp: 8 (over z, y), expert: 4 (over x, core).
Axes of the slice: x: 2, y: 2, z: 4, core: 2. Of those that a mesh axis runs over, the one named last changes fastest.
Arguments:
- tokens: bfloat16 [32768, 768], P(('dp', 'expert')), may hold values from -6 to 6
- cotangent: bfloat16 [32768, 768], P(('dp', 'expert')), may hold values from -6 to 6
- lengths: int32 [32], P(('dp', 'expert')), may hold values from 1 to 1024, 24576 in all
- adapter_ids: int32 [32], P(('dp', 'expert')), may hold values from 0 to 7
- routes: int32 [32768, 2], P(('dp', 'expert')), may hold values from 0 to 11, all different within a row; in each aligned block of 1024 rows (0 to 1023, 1024 to 2047, ...) at most 192 rows name the same one
- prev_logits: float32 [32768, 12], P(('dp', 'expert')), may hold values from -3 to 3
- norm_gains: float32 [2, 768], replicated, may hold values from 0.5 to 1.5
- input_weights: bfloat16 [3, 768, 768], replicated, may hold values from -0.21875 to 0.21875
- output_weight: bfloat16 [768, 768], replicated, may hold values from -1.25 to 1.25
- adapter_down: bfloat16 [4, 768, 128], replicated, may hold values from -0.21875 to 0.21875
- adapter_up: bfloat16 [4, 128, 768], replicated, may hold values from -0.75 to 0.75
- router: bfloat16 [768, 12], replicated, may hold values from -0.15625 to 0.15625
- residual_mix: float32 [12, 12], replicated, may hold values from -1.75 to 1.75
- constant_mix: float32 [768, 4], replicated, may hold values from -0.21875 to 0.21875
- constant_vectors: float32 [2, 768], replicated, may hold values from -5 to 5
- expert_gate: bfloat16 [8, 768, 2048], P('expert'), may hold values from -0.21875 to 0.21875
- expert_up: bfloat16 [8, 768, 2048], P('expert'), may hold values from -0.21875 to 0.21875
- expert_down: bfloat16 [8, 2048, 768], P('expert'), may hold values from -0.125 to 0.125
- expert_adapter_down: bfloat16 [8, 2, 768, 128], P('expert'), may hold values from -0.21875 to 0.21875
- expert_adapter_up: bfloat16 [8, 2, 128, 2048], P('expert'), may hold values from -0.75 to 0.75
- output_adapter_down: bfloat16 [8, 2048, 128], P('expert'), may hold values from -0.125 to 0.125
- output_adapter_up: bfloat16 [8, 128, 768], P('expert'), may hold values from -0.75 to 0.75
Outputs:
- output: bfloat16 [32768, 768], P(('dp', 'expert'))
- input_gradient: bfloat16 [32768, 768], P(('dp', 'expert'))
- adapter_down_gradient: float32 [4, 768, 128], replicated
- adapter_up_gradient: float32 [4, 128, 768], replicated
- expert_adapter_down_gradient: float32 [8, 2, 768, 128], P('expert')
- expert_adapter_up_gradient: float32 [8, 2, 128, 2048], P('expert')
- output_adapter_down_gradient: float32 [8, 2048, 128], P('expert')
- output_adapter_up_gradient: float32 [8, 128, 768], P('expert')
Inputs may be any that keep to these rules, and one draw needn't show every extreme that they name: `lengths`: each sequence's valid tokens are the first of its 1024 slots. `routes`: in the rows of one device, each expert number is named at most 192 times.
All inputs are finite; a program needn't handle non-finite values. No bound on the sum of `lengths` on one device may be relied on, other than what follows from the above.
Results may differ from a plain program's by a relative error of at most 0.015.
Values may be sent and summed in bfloat16 or wider, within the bound.
No kernel may reach another device: no remote copies, remote signals or barrier semaphores. Data moves between devices by JAX's collectives and lax.ppermute only.
A program may use at most 384 MiB of HBM per device.

v0:
```python
import math

import jax
import jax.numpy as jnp
from jax import lax
from jax.sharding import PartitionSpec as P

HEADS = 12
HD = 64
EXPERTS = 8
RANK = 16
CAP = 192


EPSILON = 1e-06
PRECISE = lax.Precision.HIGHEST


def mean_scale(value_in):
    return lax.rsqrt(jnp.mean(value_in * value_in, axis=-1, keepdims=True) + EPSILON)


def norm_back(back_normed, normed, scale):
    return scale * (back_normed - normed * jnp.mean(back_normed * normed, axis=-1, keepdims=True))


def softmax_last(value_in):
    shifted = jnp.exp(value_in - jnp.max(value_in, axis=-1, keepdims=True))
    return shifted / jnp.sum(shifted, axis=-1, keepdims=True)


def turn_tables(length_in, head_width):
    half_width = head_width // 2
    inverse = jnp.exp(
        jnp.arange(half_width, dtype=jnp.float32) * (-2.0 * math.log(10000.0) / head_width)
    )
    angles = jnp.arange(length_in, dtype=jnp.float32)[:, None] * inverse[None, :]
    angles = jnp.concatenate([angles, angles], axis=1)
    return (jnp.cos(angles), jnp.sin(angles))


def rope_turn(value_in, cosine_table, sine_table):
    half_width = value_in.shape[-1] // 2
    turned = jnp.concatenate([-value_in[..., half_width:], value_in[..., :half_width]], axis=-1)
    return value_in * cosine_table[:, None, :] + turned * sine_table[:, None, :]


def adapter_select(picked, columns):
    return (jnp.arange(columns, dtype=jnp.int32) // RANK == picked[..., None]).astype(jnp.bfloat16)


def masked_scores(queries, key_rows, seq_limit):
    positions = jnp.arange(queries.shape[0], dtype=jnp.int32)
    scores = jnp.einsum(
        "qhd,khd->hqk", queries, key_rows, preferred_element_type=jnp.float32
    ) * queries.shape[-1] ** (-0.5)
    allowed = (positions[None, :] <= positions[:, None]) & (positions[None, :] < seq_limit)
    return jnp.where(allowed[None], scores, -1e30)


def attend_one(entries):
    queries, key_rows, values, seq_limit = entries
    scores = masked_scores(queries, key_rows, seq_limit)
    row_top = jnp.max(scores, axis=-1, keepdims=True)
    shifted = jnp.exp(scores - row_top)
    row_total = jnp.sum(shifted, axis=-1, keepdims=True)
    probabilities = (shifted / row_total).astype(jnp.bfloat16)
    mixed_rows = jnp.einsum(
        "hqk,khd->qhd", probabilities, values, preferred_element_type=jnp.float32
    )
    return (mixed_rows, row_top[..., 0] + jnp.log(row_total[..., 0]))


def attend_back(entries):
    queries, key_rows, values, seq_limit, log_total, back_mixed = entries
    factor = queries.shape[-1] ** (-0.5)
    probabilities = jnp.exp(masked_scores(queries, key_rows, seq_limit) - log_total[..., None])
    back_values = jnp.einsum(
        "hqk,qhd->khd",
        probabilities.astype(jnp.bfloat16),
        back_mixed,
        preferred_element_type=jnp.float32,
    )
    back_probs = jnp.einsum("qhd,khd->hqk", back_mixed, values, preferred_element_type=jnp.float32)
    back_scores = (
        probabilities * (back_probs - jnp.sum(probabilities * back_probs, axis=-1, keepdims=True))
    ).astype(jnp.bfloat16)
    back_queries = (
        jnp.einsum("hqk,khd->qhd", back_scores, key_rows, preferred_element_type=jnp.float32)
        * factor
    )
    back_keys = (
        jnp.einsum("hqk,qhd->khd", back_scores, queries, preferred_element_type=jnp.float32)
        * factor
    )
    return (back_queries, back_keys, back_values)


def expert_forward(rows_in, picked, weights):
    gate_w, up_w, down_w, in_down, in_up, out_down, out_up = weights
    select_rows = adapter_select(picked, in_down.shape[-1])
    inner_gate = (
        jnp.einsum("erd,edk->erk", rows_in, in_down[:, 0], preferred_element_type=jnp.float32)
        * select_rows
    ).astype(jnp.bfloat16)
    gate_pre = jnp.einsum(
        "erd,edf->erf", rows_in, gate_w, preferred_element_type=jnp.float32
    ) + jnp.einsum("erk,ekf->erf", inner_gate, in_up[:, 0], preferred_element_type=jnp.float32)
    inner_up = (
        jnp.einsum("erd,edk->erk", rows_in, in_down[:, 1], preferred_element_type=jnp.float32)
        * select_rows
    ).astype(jnp.bfloat16)
    up_pre = jnp.einsum(
        "erd,edf->erf", rows_in, up_w, preferred_element_type=jnp.float32
    ) + jnp.einsum("erk,ekf->erf", inner_up, in_up[:, 1], preferred_element_type=jnp.float32)
    activated = (gate_pre * jax.nn.sigmoid(gate_pre) * up_pre).astype(jnp.bfloat16)
    inner_down = (
        jnp.einsum("erf,efk->erk", activated, out_down, preferred_element_type=jnp.float32)
        * select_rows
    ).astype(jnp.bfloat16)
    result = jnp.einsum(
        "erf,efd->erd", activated, down_w, preferred_element_type=jnp.float32
    ) + jnp.einsum("erk,ekd->erd", inner_down, out_up, preferred_element_type=jnp.float32)
    return (
        result.astype(jnp.bfloat16),
        (select_rows, inner_gate, gate_pre, inner_up, up_pre, activated, inner_down),
    )


def expert_backward(rows_in, back_result, kept, weights):
    gate_w, up_w, down_w, in_down, in_up, out_down, out_up = weights
    select_rows, inner_gate, gate_pre, inner_up, up_pre, activated, inner_down = kept
    back_inner_down = (
        jnp.einsum("erd,ekd->erk", back_result, out_up, preferred_element_type=jnp.float32).astype(
            jnp.bfloat16
        )
        * select_rows
    )
    back_out_up = jnp.einsum(
        "erk,erd->ekd", inner_down, back_result, preferred_element_type=jnp.float32
    )
    back_out_down = jnp.einsum(
        "erf,erk->efk", activated, back_inner_down, preferred_element_type=jnp.float32
    )
    back_active = jnp.einsum(
        "erd,efd->erf", back_result, down_w, preferred_element_type=jnp.float32
    ) + jnp.einsum("erk,efk->erf", back_inner_down, out_down, preferred_element_type=jnp.float32)
    sigmoid_gate = jax.nn.sigmoid(gate_pre)
    back_gate = (
        back_active * up_pre * sigmoid_gate * (1.0 + gate_pre * (1.0 - sigmoid_gate))
    ).astype(jnp.bfloat16)
    back_up = (back_active * gate_pre * sigmoid_gate).astype(jnp.bfloat16)
    back_inner_gate = (
        jnp.einsum(
            "erf,ekf->erk", back_gate, in_up[:, 0], preferred_element_type=jnp.float32
        ).astype(jnp.bfloat16)
        * select_rows
    )
    back_inner_up = (
        jnp.einsum("erf,ekf->erk", back_up, in_up[:, 1], preferred_element_type=jnp.float32).astype(
            jnp.bfloat16
        )
        * select_rows
    )
    back_in_up = jnp.stack(
        [
            jnp.einsum("erk,erf->ekf", inner_gate, back_gate, preferred_element_type=jnp.float32),
            jnp.einsum("erk,erf->ekf", inner_up, back_up, preferred_element_type=jnp.float32),
        ],
        axis=1,
    )
    back_in_down = jnp.stack(
        [
            jnp.einsum(
                "erd,erk->edk", rows_in, back_inner_gate, preferred_element_type=jnp.float32
            ),
            jnp.einsum("erd,erk->edk", rows_in, back_inner_up, preferred_element_type=jnp.float32),
        ],
        axis=1,
    )
    back_rows = jnp.einsum(
        "erf,edf->erd", back_gate, gate_w, preferred_element_type=jnp.float32
    ) + jnp.einsum("erf,edf->erd", back_up, up_w, preferred_element_type=jnp.float32)
    back_rows = (
        back_rows
        + jnp.einsum(
            "erk,edk->erd", back_inner_gate, in_down[:, 0], preferred_element_type=jnp.float32
        )
        + jnp.einsum(
            "erk,edk->erd", back_inner_up, in_down[:, 1], preferred_element_type=jnp.float32
        )
    )
    return (back_rows.astype(jnp.bfloat16), (back_in_down, back_in_up, back_out_down, back_out_up))


def body(
    tokens,
    cotangent,
    lengths,
    adapter_ids,
    routes,
    prev_logits,
    norm_gains,
    input_weights,
    output_weight,
    adapter_down,
    adapter_up,
    router,
    residual_mix,
    constant_mix,
    constant_vectors,
    expert_gate,
    expert_up,
    expert_down,
    expert_adapter_down,
    expert_adapter_up,
    output_adapter_down,
    output_adapter_up,
):
    tok_count, model_width = tokens.shape
    seq_count = lengths.shape[0]
    seq_slots = tok_count // seq_count
    positions = jnp.arange(seq_slots, dtype=jnp.int32)
    valid = (positions[None, :] < lengths[:, None]).reshape(-1).astype(jnp.float32)
    row_adapter = jnp.repeat(adapter_ids, seq_slots)
    select_all = adapter_select(row_adapter, adapter_down.shape[-1])
    cosine_table, sine_table = turn_tables(seq_slots, HD)
    head_shape = (seq_count, seq_slots, HEADS, HD)

    def project(source_rows, weight, index):
        inner = (
            jnp.dot(source_rows, adapter_down[index], preferred_element_type=jnp.float32)
            * select_all
        ).astype(jnp.bfloat16)
        return (
            jnp.dot(source_rows, weight, preferred_element_type=jnp.float32)
            + jnp.dot(inner, adapter_up[index], preferred_element_type=jnp.float32),
            inner,
        )

    def project_back(back_value, source_rows, inner, weight, index):
        back_inner = (
            jnp.dot(back_value, adapter_up[index].T, preferred_element_type=jnp.float32).astype(
                jnp.bfloat16
            )
            * select_all
        )
        back_source = jnp.dot(back_value, weight.T, preferred_element_type=jnp.float32) + jnp.dot(
            back_inner, adapter_down[index].T, preferred_element_type=jnp.float32
        )
        back_down = jnp.dot(source_rows.T, back_inner, preferred_element_type=jnp.float32)
        back_upper = jnp.dot(inner.T, back_value, preferred_element_type=jnp.float32)
        return (back_source, back_down, back_upper)

    x_float = tokens.astype(jnp.float32)
    scale_first = mean_scale(x_float)
    normed_first = x_float * scale_first
    normed_rows = (normed_first * norm_gains[0]).astype(jnp.bfloat16)
    queries, inner_query = project(normed_rows, input_weights[0], 0)
    key_rows, inner_key = project(normed_rows, input_weights[1], 1)
    values, inner_value = project(normed_rows, input_weights[2], 2)
    turned_q = rope_turn(queries.reshape(head_shape), cosine_table, sine_table).astype(jnp.bfloat16)
    turned_k = rope_turn(key_rows.reshape(head_shape), cosine_table, sine_table).astype(
        jnp.bfloat16
    )
    values_rows = values.reshape(head_shape).astype(jnp.bfloat16)
    mixed_rows, log_total = lax.map(attend_one, (turned_q, turned_k, values_rows, lengths))
    mixed_flat = mixed_rows.reshape(tok_count, model_width).astype(jnp.bfloat16)
    attention_out, inner_output = project(mixed_flat, output_weight, 3)
    hidden = x_float + attention_out
    scale_second = mean_scale(hidden)
    normed_second = hidden * scale_second
    expert_rows = (normed_second * norm_gains[1]).astype(jnp.bfloat16)
    expert_float = expert_rows.astype(jnp.float32)
    logits = jnp.dot(expert_rows, router, preferred_element_type=jnp.float32) + jnp.dot(
        prev_logits, residual_mix, precision=PRECISE
    )
    route_hot = (routes[..., None] == jnp.arange(EXPERTS + 4, dtype=jnp.int32)).astype(jnp.float32)
    gates = softmax_last(jnp.sum(route_hot * logits[:, None, :], axis=-1))
    const_w = softmax_last(
        jnp.dot(expert_float, constant_mix, precision=PRECISE).reshape(tok_count, 2, 2)
    )
    const_out = (
        const_w[..., 0:1] * expert_float[:, None, :] + const_w[..., 1:2] * constant_vectors[None]
    )
    copy_hot = (routes == EXPERTS + 1).astype(jnp.float32)
    const_hot = (routes[..., None] == EXPERTS + 2 + jnp.arange(2, dtype=jnp.int32)).astype(
        jnp.float32
    )
    local = (
        copy_hot[..., None] * expert_float[:, None, :]
        + const_hot[..., 0:1] * const_out[:, None, 0]
        + const_hot[..., 1:2] * const_out[:, None, 1]
    )
    group_size = lax.axis_size("expert")
    local_experts = expert_gate.shape[0]
    live_rows = ((routes < EXPERTS) & (valid[:, None] > 0)).reshape(-1)
    flat_route = routes.reshape(-1)
    route_hits = (
        (flat_route[:, None] == jnp.arange(EXPERTS, dtype=jnp.int32)[None, :]) & live_rows[:, None]
    ).astype(jnp.int32)
    slot_index = jnp.sum((jnp.cumsum(route_hits, axis=0) - 1) * route_hits, axis=1)
    slot_spaces = EXPERTS * CAP
    target = (
        flat_route % local_experts * (group_size * CAP)
        + flat_route // local_experts * CAP
        + slot_index
    )
    target = jnp.where(live_rows, target, slot_spaces)
    source = (
        jnp.zeros(slot_spaces + 1, jnp.int32)
        .at[target]
        .set(jnp.arange(tok_count * 2, dtype=jnp.int32))[:slot_spaces]
    )
    filled = jnp.zeros(slot_spaces + 1, jnp.float32).at[target].set(1.0)[:slot_spaces]
    slot_rows = source // 2
    send_rows = expert_rows[slot_rows] * filled[:, None].astype(jnp.bfloat16)
    send_ids = row_adapter[slot_rows]
    expert_weights = (
        expert_gate,
        expert_up,
        expert_down,
        expert_adapter_down,
        expert_adapter_up,
        output_adapter_down,
        output_adapter_up,
    )
    owner_shape = (local_experts, group_size, CAP, model_width)
    got_rows, got_ids = (
        lax.all_to_all(
            send_rows.reshape(owner_shape), "expert", split_axis=1, concat_axis=1, tiled=True
        ),
        lax.all_to_all(
            send_ids.reshape(local_experts, group_size, CAP),
            "expert",
            split_axis=1,
            concat_axis=1,
            tiled=True,
        ),
    )
    rows_in = got_rows.reshape(local_experts, group_size * CAP, model_width)
    rows_ids = got_ids.reshape(local_experts, group_size * CAP)
    result_rows, kept = expert_forward(rows_in, rows_ids, expert_weights)
    back_flat = lax.all_to_all(
        result_rows.reshape(owner_shape), "expert", split_axis=1, concat_axis=1, tiled=True
    ).reshape(slot_spaces, model_width)
    padded_back = jnp.concatenate(
        [back_flat.astype(jnp.float32), jnp.zeros((1, model_width), jnp.float32)], axis=0
    )
    outputs_all = padded_back[target].reshape(tok_count, 2, model_width) + local
    mixture = valid[:, None] * jnp.sum(gates[..., None] * outputs_all, axis=1)
    layer_out = (hidden + mixture).astype(jnp.bfloat16)
    back_out = cotangent.astype(jnp.float32) * valid[:, None]
    back_gates = jnp.sum(back_out[:, None, :] * outputs_all, axis=-1)
    back_chosen = gates * (back_gates - jnp.sum(gates * back_gates, axis=1, keepdims=True))
    back_logits = jnp.sum(route_hot * back_chosen[..., None], axis=1)
    back_expert = jnp.dot(back_logits, router.astype(jnp.float32).T, precision=PRECISE)
    back_outputs = gates[..., None] * back_out[:, None, :]
    back_expert = back_expert + jnp.sum(copy_hot[..., None] * back_outputs, axis=1)
    back_const = (
        const_hot[:, 0, :, None] * back_outputs[:, 0:1, :]
        + const_hot[:, 1, :, None] * back_outputs[:, 1:2, :]
    )
    back_weight = jnp.stack(
        [
            jnp.sum(back_const * expert_float[:, None, :], axis=-1),
            jnp.sum(back_const * constant_vectors[None], axis=-1),
        ],
        axis=-1,
    )
    back_mix = const_w * (back_weight - jnp.sum(const_w * back_weight, axis=-1, keepdims=True))
    back_expert = (
        back_expert
        + jnp.sum(const_w[..., 0:1] * back_const, axis=1)
        + jnp.dot(back_mix.reshape(tok_count, 4), constant_mix.T, precision=PRECISE)
    )
    back_send = (back_out[slot_rows] * (gates.reshape(-1)[source] * filled)[:, None]).astype(
        jnp.bfloat16
    )
    back_result = lax.all_to_all(
        back_send.reshape(owner_shape), "expert", split_axis=1, concat_axis=1, tiled=True
    ).reshape(local_experts, group_size * CAP, model_width)
    back_rows, expert_grads = expert_backward(rows_in, back_result, kept, expert_weights)
    back_rows_flat = lax.all_to_all(
        back_rows.reshape(owner_shape), "expert", split_axis=1, concat_axis=1, tiled=True
    ).reshape(slot_spaces, model_width)
    expert_sums = lax.psum(
        (expert_grads[0], expert_grads[1], expert_grads[2], expert_grads[3]), "dp"
    )
    padded_rows = jnp.concatenate(
        [back_rows_flat.astype(jnp.float32), jnp.zeros((1, model_width), jnp.float32)], axis=0
    )
    back_expert = back_expert + jnp.sum(
        padded_rows[target].reshape(tok_count, 2, model_width), axis=1
    )
    back_hidden = back_out + norm_back(back_expert * norm_gains[1], normed_second, scale_second)
    back_attention = back_hidden.astype(jnp.bfloat16)
    back_mixed, down_output, upper_output = project_back(
        back_attention, mixed_flat, inner_output, output_weight, 3
    )
    back_mixed_rows = back_mixed.reshape(head_shape).astype(jnp.bfloat16)
    back_turned_q, back_turned_k, back_values = lax.map(
        attend_back, (turned_q, turned_k, values_rows, lengths, log_total, back_mixed_rows)
    )
    back_query = (
        rope_turn(back_turned_q, cosine_table, -sine_table)
        .reshape(tok_count, model_width)
        .astype(jnp.bfloat16)
    )
    back_key = (
        rope_turn(back_turned_k, cosine_table, -sine_table)
        .reshape(tok_count, model_width)
        .astype(jnp.bfloat16)
    )
    back_value = back_values.reshape(tok_count, model_width).astype(jnp.bfloat16)
    source_query, down_query, upper_query = project_back(
        back_query, normed_rows, inner_query, input_weights[0], 0
    )
    source_key, down_key, upper_key = project_back(
        back_key, normed_rows, inner_key, input_weights[1], 1
    )
    source_value, down_value, upper_value = project_back(
        back_value, normed_rows, inner_value, input_weights[2], 2
    )
    back_normed = source_query + source_key + source_value
    input_back = (
        back_hidden + norm_back(back_normed * norm_gains[0], normed_first, scale_first)
    ).astype(jnp.bfloat16)
    adapter_sums = lax.psum(
        (
            jnp.stack([down_query, down_key, down_value, down_output]),
            jnp.stack([upper_query, upper_key, upper_value, upper_output]),
        ),
        ("dp", "expert"),
    )
    return (
        layer_out,
        input_back,
        adapter_sums[0],
        adapter_sums[1],
        expert_sums[0],
        expert_sums[1],
        expert_sums[2],
        expert_sums[3],
    )


def solution(mesh):
    placed = (
        P(("dp", "expert"), None),
        P(("dp", "expert"), None),
        P(("dp", "expert")),
        P(("dp", "expert")),
        P(("dp", "expert"), None),
        P(("dp", "expert"), None),
        P(),
        P(),
        P(),
        P(),
        P(),
        P(),
        P(),
        P(),
        P(),
        P("expert", None, None),
        P("expert", None, None),
        P("expert", None, None),
        P("expert", None, None, None),
        P("expert", None, None, None),
        P("expert", None, None),
        P("expert", None, None),
    )
    return jax.shard_map(
        body,
        mesh=mesh,
        in_specs=placed,
        out_specs=(
            P(("dp", "expert"), None),
            P(("dp", "expert"), None),
            P(),
            P(),
            P("expert", None, None, None),
            P("expert", None, None, None),
            P("expert", None, None),
            P("expert", None, None),
        ),
        check_vma=False,
    )
```

profile of v0, /device:TPU:0, one launch (start us, length us, event | category | flops | bytes accessed | tf_op | source)
XLA Modules:
  0.0 930.7 jit_solution(5813527786861601140)
XLA Ops:
  16.0 8.0 scatter_custom_fusion
  24.7 5.9 gather_fusion.1
  31.3 4.7 all-to-all-start.1
  57.3 22.4 %fusion.6 = (f32[12,1024]{1,0:T(8,128)}, f32[12,1024,1024]{1,2,0:T(8,128)}) fusion(pred[1024,1024]{0,1:T(8,128)(4,1)} %fusion.11, bf16[1024,12,64]{0,2,1:T(8,128)(2,1)} %get-tuple-element.150, bf16[1024,12,64]{0,2,1:T(8,128)(2,1)} %get-tuple-element.149), kind=kOutput, calls=%fused_computation.19 | convolution fusion | flops 1648349184 | bytes 54575104 | tf_op jit(solution)/shard_map/while/body/eval_jaxpr/qhd,khd->hqk/dot_general | solution.py:54
  79.7 21.7 %fusion = f32[12,1024]{1,0:T(8,128)S(1)} fusion(f32[12,1024]{1,0:T(8,128)} %get-tuple-element.165, f32[12,1024,1024]{1,2,0:T(8,128)} %get-tuple-element.166, pred[1024,1024]{0,1:T(8,128)(4,1)} %fusion.11), kind=kLoop, calls=%fused_computation.14 | loop fusion | flops 50319360 | bytes 51478528 | tf_op jit(solution)/shard_map/while/body/eval_jaxpr/reduce_sum | solution.py:66
  102.7 20.3 %fusion.32 = bf16[12,64,1024]{2,1,0:T(8,128)(2,1)S(1)} fusion(bf16[1024,12,64]{0,2,1:T(8,128)(2,1)S(1)} %bitcast.351, f32[12,1024]{1,0:T(8,128)S(1)} %fusion, f32[12,1024]{1,0:T(8,128)S(1)} %copy-done.66, f32[12,1024,1024]{1,2,0:T(8,128)} %get-tuple-element.166, pred[1024,1024]{0,1:T(8,128)(4,1)S(1)} %copy-done.3), kind=kOutput, calls=%fused_computation.95 | convolution fusion | flops 1674313728 | bytes 54624256 | tf_op jit(solution)/shard_map/while/body/eval_jaxpr/hqk,khd->qhd/dot_general | solution.py:68
  135.3 5.7 gather_fusion
  141.0 8.2 scatter_custom_fusion.1
  162.9 8.2 broadcast_multiply_fusion
  171.1 12.7 %fusion.152 = (f32[1024,1,768]{2,1,0:T(1,128)}, f32[1024,1,768]{2,1,0:T(1,128)}) fusion(f32[1024,2,768]{2,1,0:T(2,128)} %broadcast_multiply_fusion), kind=kLoop, calls=%fused_computation.313 | loop fusion | bytes 12582912 | tf_op jit(solution)/shard_map/slice | solution.py:361
  183.9 4.0 copy.416
  190.3 39.2 %multiply_reduce_fusion.2 = (f32[1024,2]{1,0:T(8,128)}, f32[1024,2]{1,0:T(8,128)}, f32[1024,768]{1,0:T(8,128)}, f32[1024,2,768]{2,1,0:T(2,128)}) fusion(f32[1024,768]{1,0:T(8,128)} %bitcast.337, f32[1024,2]{1,0:T(8,128)S(1)} %copy.359, f32[1024,768]{1,0:T(8,128)} %bitcast.338, f32[1024,2]{1,0:T(8,128)S(1)} %copy.358, f32[1024,768]{1,0:T(8,128)} %copy.347, ...), kind=kLoop, calls=%fused_computation.25 | loop fusion | flops 18083840 | bytes 18929664 | tf_op jit(solution)/shard_map/reduce_sum | solution.py:366
  229.5 12.9 %fusion.153 = (f32[1024,1,768]{2,1,0:T(1,128)}, f32[1024,1,768]{2,1,0:T(1,128)}) fusion(f32[1024,2,768]{2,1,0:T(2,128)} %get-tuple-element.136), kind=kLoop, calls=%fused_computation.314 | loop fusion | bytes 12582912 | tf_op jit(solution)/shard_map/slice | solution.py:292
  249.9 8.8 gather_fusion.3
  258.7 11.9 %gather_fusion.4 = f32[1536]{0:T(1024)} fusion(f32[2048]{0:T(1024)S(1)} %div.111, s32[2048]{0:T(1024)} %pad_clamp_fusion), kind=kCustom, calls=%fused_computation.4 | custom fusion | bytes 18432 | tf_op jit(solution)/shard_map/gather | solution.py:377
  301.7 4.1 fusion.7
  308.5 4.7 all-to-all-start.3
  315.1 10.8 %fusion.158 = f32[2,768,2048]{2,1,0:T(8,128)} fusion(bf16[2,768,768]{2,1,0:T(8,128)(2,1)S(1)} %bitcast.324, bf16[2,768,2048]{2,1,0:T(8,128)(2,1)} %param.37), kind=kOutput, calls=%fused_computation.319 | convolution fusion | flops 4831838208 | bytes 21233664 | tf_op jit(solution)/shard_map/erd,edf->erf/dot_general | solution.py:106
  328.9 10.7 %fusion.159 = f32[2,768,2048]{2,1,0:T(8,128)} fusion(bf16[2,768,768]{2,1,0:T(8,128)(2,1)S(1)} %bitcast.327, bf16[2,768,2048]{2,1,0:T(8,128)(2,1)} %param.38), kind=kOutput, calls=%fused_computation.320 | convolution fusion | flops 4831838208 | bytes 21233664 | tf_op jit(solution)/shard_map/erd,edf->erf/dot_general | solution.py:113
  344.5 10.9 %fusion.163 = f32[2,768,2048]{2,1,0:T(8,128)} fusion(bf16[2,768,768]{2,1,0:T(8,128)(2,1)S(1)} %bitcast.343, bf16[2,2048,768]{2,1,0:T(8,128)(2,1)} %param.39), kind=kOutput, calls=%fused_computation.324 | convolution fusion | flops 4831838208 | bytes 21233664 | tf_op jit(solution)/shard_map/erd,efd->erf/dot_general | solution.py:145
  355.5 6.3 fusion.61
  361.8 6.4 fusion.164
  368.2 29.6 %multiply_convert_fusion.1 = (bf16[2,768,2048]{2,1,0:T(8,128)(2,1)}, bf16[2,768,2048]{2,1,0:T(8,128)(2,1)}, bf16[2,768,2048]{2,1,0:T(8,128)(2,1)}) fusion(f32[2,768,2048]{2,1,0:T(8,128)} %fusion.163, f32[2,768,2048]{2,1,0:T(8,128)} %fusion.164, f32[2,768,2048]{2,1,0:T(8,128)} %fusion.159, f32[2,768,2048]{2,1,0:T(8,128)} %fusion.61, ...), kind=kOutput, calls=%fused_computation.20 | convolution fusion | flops 865075200 | bytes 83230720 | tf_op jit(solution)/shard_map/erk,ekf->erf/dot_general | solution.py:108
  397.9 5.0 fusion.37
  403.0 9.1 fusion.160
  418.8 10.0 %fusion.165 = f32[2,768,768]{2,1,0:T(8,128)} fusion(bf16[2,768,2048]{2,1,0:T(8,128)(2,1)S(1)} %bitcast.332, bf16[2,768,2048]{2,1,0:T(8,128)(2,1)} %param.37), kind=kOutput, calls=%fused_computation.326 | convolution fusion | flops 4831838208 | bytes 17301504 | tf_op jit(solution)/shard_map/erf,edf->erd/dot_general | solution.py:181
  430.7 9.6 %fusion.166 = f32[2,768,768]{2,1,0:T(8,128)} fusion(bf16[2,768,2048]{2,1,0:T(8,128)(2,1)S(1)} %bitcast.336, bf16[2,768,2048]{2,1,0:T(8,128)(2,1)} %param.38), kind=kOutput, calls=%fused_computation.327 | convolution fusion | flops 4831838208 | bytes 17301504 | tf_op jit(solution)/shard_map/erf,edf->erd/dot_general | solution.py:183
  449.7 6.1 add_convert_fusion
  459.3 4.3 convolution_bitcast_fusion
  470.9 7.2 all-to-all-done.2
  478.2 4.5 all-to-all-start.4
  485.6 13.0 %gather_fusion.2 = f32[2048,768]{1,0:T(8,128)} fusion(f32[1537,768]{1,0:T(8,128)} %pad_convert_fusion.1, s32[2048]{0:T(1024)S(1)} %broadcast_clamp_fusion), kind=kCustom, calls=%fused_computation.2 | custom fusion | bytes 12591104 | tf_op jit(solution)/shard_map/gather | solution.py:350
  498.5 8.3 reshape.668
  506.9 40.3 %multiply_reduce_fusion.5 = (f32[1024,2]{1,0:T(8,128)}, f32[1024,768]{1,0:T(8,128)}, f32[1024,768]{1,0:T(8,128)}) fusion(f32[1024,768]{1,0:T(8,128)} %copy.354, f32[1024,2]{1,0:T(8,128)S(1)} %copy-done.23, f32[1024,2]{1,0:T(8,128)S(1)} %copy-done.37, f32[1024,2,768]{2,1,0:T(2,128)} %reshape.668, f32[1024,768]{1,0:T(8,128)} %bitcast.339, ...), kind=kLoop, calls=%fused_computation.29 | loop fusion | flops 18872320 | bytes 25206784 | tf_op jit(solution)/shard_map/reduce_sum | solution.py:354
  559.7 13.0 %gather_fusion.5 = f32[2048,768]{1,0:T(8,128)} fusion(f32[1537,768]{1,0:T(8,128)} %pad_convert_fusion, s32[2048]{0:T(1024)S(1)} %broadcast_clamp_fusion), kind=kCustom, calls=%fused_computation.5 | custom fusion | bytes 12591104 | tf_op jit(solution)/shard_map/gather | solution.py:394
  572.8 8.4 reshape.672
  581.1 12.5 %reduce_sum.201 = f32[1024,768]{1,0:T(8,128)} reduce(f32[1024,2,768]{2,1,0:T(2,128)} %reshape.672, f32[]{:T(128)} %constant.133.clone.1), dimensions={1}, to_apply=%region_23.24 | reduce | flops 786432 | bytes 9437188 | tf_op jit(solution)/shard_map/reduce_sum | solution.py:393
  597.3 8.9 multiply_reduce_fusion.7
  606.2 4.1 copy.352
  610.3 6.3 multiply_add_fusion.2
  622.7 35.3 %multiply_reduce_fusion = (f32[12,1024]{1,0:T(8,128)S(1)}, f32[12,1024,1024]{1,2,0:T(8,128)}) fusion(f32[12,1024]{1,0:T(8,128)S(1)} %copy-done.52, f32[12,1024,1024]{1,2,0:T(8,128)} %get-tuple-element.166, pred[1024,1024]{0,1:T(8,128)(4,1)S(1)} %copy-done.4, bf16[1024,12,64]{0,2,1:T(8,128)(2,1)} %bitcast.359, bf16[1024,12,64]{0,2,1:T(8,128)(2,1)} %bitcast.352), kind=kOutput, calls=%fused_computation.9 | convolution fusion | flops 1673515008 | bytes 104955904 | tf_op jit(solution)/shard_map/while/body/eval_jaxpr/qhd,khd->hqk/dot_general | solution.py:84
  658.0 41.9 %multiply_convert_fusion = bf16[12,1024,1024]{1,2,0:T(8,128)(2,1)} fusion(f32[12,1024,1024]{1,2,0:T(8,128)} %get-tuple-element.172, f32[12,1024]{1,0:T(8,128)S(1)} %get-tuple-element.171, f32[12,1024]{1,0:T(8,128)S(1)} %copy-done.52, f32[12,1024,1024]{1,2,0:T(8,128)} %get-tuple-element.166, pred[1024,1024]{0,1:T(8,128)(4,1)S(1)} %copy-done.4), kind=kLoop, calls=%fused_computation.8 | loop fusion | flops 75497472 | bytes 126976000 | tf_op jit(solution)/shard_map/while/body/eval_jaxpr/convert_element_type | solution.py:87
  699.9 14.5 %fusion.168 = f32[12,64,1024]{2,1,0:T(8,128)} fusion(bf16[1024,12,64]{0,2,1:T(8,128)(2,1)} %get-tuple-element.150, bf16[12,1024,1024]{1,2,0:T(8,128)(2,1)} %multiply_convert_fusion), kind=kOutput, calls=%fused_computation.329 | convolution fusion | flops 1610612736 | bytes 29884416 | tf_op jit(solution)/shard_map/while/body/eval_jaxpr/hqk,qhd->khd/dot_general | solution.py:93
  714.4 11.4 %fusion.167 = f32[12,64,1024]{2,1,0:T(8,128)S(1)} fusion(bf16[1024,12,64]{0,2,1:T(8,128)(2,1)} %get-tuple-element.149, bf16[12,1024,1024]{1,2,0:T(8,128)(2,1)} %multiply_convert_fusion), kind=kOutput, calls=%fused_computation.328 | convolution fusion | flops 1610612736 | bytes 29884416 | tf_op jit(solution)/shard_map/while/body/eval_jaxpr/hqk,khd->qhd/dot_general | solution.py:89
  732.6 21.3 %fusion.29 = bf16[12,64,1024]{2,1,0:T(8,128)(2,1)} fusion(bf16[1024,12,64]{0,2,1:T(8,128)(2,1)S(1)} %bitcast.360, f32[12,1024]{1,0:T(8,128)S(1)} %copy-done.52, f32[12,1024,1024]{1,2,0:T(8,128)} %get-tuple-element.166, pred[1024,1024]{0,1:T(8,128)(4,1)S(1)} %copy-done.4), kind=kOutput, calls=%fused_computation.94 | convolution fusion | flops 1661730816 | bytes 54575104 | tf_op jit(solution)/shard_map/while/body/eval_jaxpr/hqk,qhd->khd/dot_general | solution.py:78
  779.8 5.4 fusion.13
  791.7 4.8 copy.383
  797.8 119.7 %all-reduce.7.cloned.1.call-done = (f32[4,768,128]{2,1,0:T(8,128)}, f32[4,128,768]{2,1,0:T(8,128)}) async-done(((f32[4,768,128]{2,1,0:T(8,128)}, f32[4,128,768]{2,1,0:T(8,128)}), (f32[4,768,128]{2,1,0:T(8,128)}, f32[4,128,768]{2,1,0:T(8,128)})) %all-reduce.7.cloned.1.call-update) | async-done | bytes 3145744 | tf_op jit(solution)/shard_map/psum | solution.py:429
  (446 shorter events, 210.2 us)
Async XLA Ops:
  7.2 117.7 %copy-start = (bf16[768,768]{1,0:T(8,128)(2,1)S(1)}, bf16[768,768]{1,0:T(8,128)(2,1)}, u32[]{:S(2)}) copy-start(bf16[768,768]{1,0:T(8,128)(2,1)} %param.30) | copy-start | bytes 3538948
  16.0 14.6 %copy-start.108 = (s32[2048,1]{0,1:T(1,128)}, s32[2048,1]{0,1:T(1,128)S(1)}, u32[]{:S(2)}) copy-start(s32[2048,1]{0,1:T(1,128)S(1)} %compare_select_fusion.3) | copy-start | bytes 24580
  24.7 110.5 %copy-start.80 = (s32[2048]{0:T(1024)}, s32[2048]{0:T(1024)S(1)}, u32[]{:S(2)}) copy-start(s32[2048]{0:T(1024)S(1)} %pad_clamp_fusion.1) | copy-start | bytes 24580
  31.3 212.8 %all-to-all-start.1 = ((s32[2,4,192]{2,0,1:T(2,128)}), s32[2,4,192]{2,0,1:T(2,128)}, u32[]{:S(2)}, u32[]{:S(2)}) async-start(s32[2,4,192]{2,0,1:T(2,128)} %copy.339), calls=%async_computation.1 | async-start | bytes 16384 | tf_op jit(solution)/shard_map/all_to_all | solution.py:333
  37.8 88.6 %copy-start.1 = (bf16[1024,768]{0,1:T(8,128)(2,1)}, bf16[1024,768]{0,1:T(8,128)(2,1)S(1)}, u32[]{:S(2)}) copy-start(bf16[1024,768]{0,1:T(8,128)(2,1)S(1)} %copy.325) | copy-start | bytes 4718596
  38.2 89.1 %copy-start.100 = (f32[768]{0:T(1024)}, f32[768]{0:T(1024)S(1)}, u32[]{:S(2)}) copy-start(f32[768]{0:T(1024)S(1)} %get-tuple-element.121) | copy-start | bytes 9220
  40.1 8.8 copy-start.58
  41.5 8.5 copy-start.56
  79.7 21.7 %copy-start.34 = (f32[1024,768]{0,1:T(8,128)S(1)}, f32[1024,768]{0,1:T(8,128)}, u32[]{:S(2)}) copy-start(f32[1024,768]{0,1:T(8,128)} %fusion.54) | copy-start | bytes 9437188
  79.7 21.7 %copy-start.55 = (bf16[1024,128]{1,0:T(8,128)(2,1)S(1)}, bf16[1024,128]{1,0:T(8,128)(2,1)}, u32[]{:S(2)}) copy-start(bf16[1024,128]{1,0:T(8,128)(2,1)} %fusion.40) | copy-start | bytes 786436
  101.5 21.6 %copy-start.74 = (f32[12,1024]{1,0:T(8,128)}, f32[12,1024]{1,0:T(8,128)S(1)}, u32[]{:S(2)}) copy-start(f32[12,1024]{1,0:T(8,128)S(1)} %fusion) | copy-start | bytes 147460
  102.1 20.9 %copy-start.27 = (bf16[1024,768]{0,1:T(8,128)(2,1)}, bf16[1024,768]{0,1:T(8,128)(2,1)S(1)}, u32[]{:S(2)}) copy-start(bf16[1024,768]{0,1:T(8,128)(2,1)S(1)} %add_convert_fusion.4) | copy-start | bytes 4718596
  102.7 20.3 %copy-start.117 = (f32[128]{0:T(128)S(1)}, f32[128]{0:T(128)}, u32[]{:S(2)}) copy-start(f32[128]{0:T(128)} %copy-done.116) | copy-start | bytes 1540
  135.3 14.0 %copy-start.90 = (f32[1024,12]{0,1:T(8,128)S(1)}, f32[1024,12]{0,1:T(8,128)}, u32[]{:S(2)}) copy-start(f32[1024,12]{0,1:T(8,128)} %param.27) | copy-start | bytes 147460
  135.3 14.0 %copy-start.109 = (f32[12,12]{1,0:T(8,128)S(1)}, f32[12,12]{1,0:T(8,128)}, u32[]{:S(2)}) copy-start(f32[12,12]{1,0:T(8,128)} %param.34) | copy-start | bytes 1732
  135.3 14.5 %copy-start.85 = (bf16[768,12]{0,1:T(8,128)(2,1)S(1)}, bf16[768,12]{0,1:T(8,128)(2,1)}, u32[]{:S(2)}) copy-start(bf16[768,12]{0,1:T(8,128)(2,1)} %param.33) | copy-start | bytes 55300
  135.3 16.2 %copy-start.75 = (s32[1024,2]{0,1:T(2,128)S(1)}, s32[1024,2]{0,1:T(2,128)}, u32[]{:S(2)}) copy-start(s32[1024,2]{0,1:T(2,128)} %param.26) | copy-start | bytes 24580
  151.9 11.0 %copy-start.22 = (f32[1024,2]{1,0:T(8,128)}, f32[1024,2]{1,0:T(8,128)S(1)}, u32[]{:S(2)}) copy-start(f32[1024,2]{1,0:T(8,128)S(1)} %copy.327) | copy-start | bytes 24580
  161.8 9.3 %copy-start.77 = (f32[1024,4]{0,1:T(4,128)}, f32[1024,4]{0,1:T(4,128)S(1)}, u32[]{:S(2)}) copy-start(f32[1024,4]{0,1:T(4,128)S(1)} %fusion.161) | copy-start | bytes 49156
  162.0 9.2 copy-start.81
  189.8 39.7 %copy-start.79 = (f32[1024,2,2]{0,2,1:T(2,128)}, f32[1024,2,2]{0,2,1:T(2,128)S(1)}, u32[]{:S(2)}) copy-start(f32[1024,2,2]{0,2,1:T(2,128)S(1)} %compare_convert_fusion.1) | copy-start | bytes 49156
  229.5 12.9 %copy-start.18 = (bf16[1536,768]{1,0:T(8,128)(2,1)S(1)}, bf16[1536,768]{1,0:T(8,128)(2,1)}, u32[]{:S(2)}) copy-start(bf16[1536,768]{1,0:T(8,128)(2,1)} %gather_fusion) | copy-start | bytes 7077892
  244.1 63.0 %all-to-all-start = ((bf16[2,4,192,768]{3,2,0,1:T(8,128)(2,1)}), bf16[2,4,192,768]{3,2,0,1:T(8,128)(2,1)S(1)}, u32[]{:S(2)}, u32[]{:S(2)}) async-start(bf16[2,4,192,768]{3,2,0,1:T(8,128)(2,1)} %copy_multiply_fusion.1), calls=%async_computation | async-start | bytes 4718592 | tf_op jit(solution)/shard_map/all_to_all | solution.py:330
  308.5 33.3 %all-to-all-start.3 = ((bf16[2,4,192,768]{3,2,0,1:T(8,128)(2,1)}), bf16[2,4,192,768]{3,2,0,1:T(8,128)(2,1)}, u32[]{:S(2)}, u32[]{:S(2)}) async-start(bf16[2,4,192,768]{3,2,0,1:T(8,128)(2,1)} %fusion.7), calls=%async_computation.3 | async-start | bytes 4718592 | tf_op jit(solution)/shard_map/all_to_all | solution.py:380
  315.0 10.8 %copy-start.64 = (bf16[2,2,768,128]{3,2,1,0:T(8,128)(2,1)S(1)}, bf16[2,2,768,128]{3,2,1,0:T(8,128)(2,1)}, u32[]{:S(2)}) copy-start(bf16[2,2,768,128]{3,2,1,0:T(8,128)(2,1)} %param.40) | copy-start | bytes 2359300
  315.0 10.8 %copy-start.112 = (s32[2,768]{1,0:T(2,128)S(1)}, s32[2,768]{1,0:T(2,128)}, u32[]{:S(2)}) copy-start(s32[2,768]{1,0:T(2,128)} %eq.105) | copy-start | bytes 18436
  315.0 10.8 %copy-start.118 = (s32[128]{0:T(128)S(1)}, s32[128]{0:T(128)}, u32[]{:S(2)}) copy-start(s32[128]{0:T(128)} %and_select_fusion.2) | copy-start | bytes 1540
  343.7 11.8 %copy-start.20 = (bf16[2,4,192,768]{3,2,1,0:T(8,128)(2,1)}, bf16[2,4,192,768]{3,2,1,0:T(8,128)(2,1)S(1)}, u32[]{:S(2)}) copy-start(bf16[2,4,192,768]{3,2,1,0:T(8,128)(2,1)S(1)} %copy.367) | copy-start | bytes 7077892
  344.5 17.3 %copy-start.41 = (bf16[2,768,128]{2,1,0:T(8,128)(2,1)}, bf16[2,768,128]{2,1,0:T(8,128)(2,1)S(1)}, u32[]{:S(2)}) copy-start(bf16[2,768,128]{2,1,0:T(8,128)(2,1)S(1)} %compare_select_fusion.2) | copy-start | bytes 1179652
  344.5 11.0 %copy-start.24 = (bf16[2,768,128]{2,1,0:T(8,128)(2,1)S(1)}, bf16[2,768,128]{2,1,0:T(8,128)(2,1)}, u32[]{:S(2)}) copy-start(bf16[2,768,128]{2,1,0:T(8,128)(2,1)} %fusion.39) | copy-start | bytes 1179652
  344.5 11.0 %copy-start.67 = (bf16[2,2,128,2048]{3,2,1,0:T(8,128)(2,1)S(1)}, bf16[2,2,128,2048]{3,2,1,0:T(8,128)(2,1)}, u32[]{:S(2)}) copy-start(bf16[2,2,128,2048]{3,2,1,0:T(8,128)(2,1)} %param.41) | copy-start | bytes 6291460
  397.9 14.2 %slice-start = ((s8[6291456]{0:T(1024)(128)(4,1)}), s8[4194304]{0:T(1024)(128)(4,1)S(1)}, s32[]{:S(2)}) async-start(s8[6291456]{0:T(1024)(128)(4,1)} %bitcast.331), calls=%async_computation.7 | async-start | bytes 8388608
  402.9 9.2 slice-start.1
  402.9 9.2 copy-start.68
  403.0 9.2 copy-start.120
  415.9 13.0 %slice-start.4 = ((s8[6291456]{0:T(1024)(128)(4,1)}), s8[4194304]{0:T(1024)(128)(4,1)S(1)}, s32[]{:S(2)}) async-start(s8[6291456]{0:T(1024)(128)(4,1)} %bitcast.335), calls=%async_computation.11 | async-start | bytes 8388608
  418.8 10.1 %slice-start.5 = ((s8[6291456]{0:T(1024)(128)(4,1)}), s8[2097152]{0:T(1024)(128)(4,1)S(1)}, s32[]{:S(2)}) async-start(s8[6291456]{0:T(1024)(128)(4,1)} %bitcast.335), calls=%async_computation.12 | async-start | bytes 4194304
  430.7 9.6 %copy-start.49 = (bf16[2,768,128]{2,1,0:T(8,128)(2,1)}, bf16[2,768,128]{2,1,0:T(8,128)(2,1)S(1)}, u32[]{:S(2)}) copy-start(bf16[2,768,128]{2,1,0:T(8,128)(2,1)S(1)} %compare_select_fusion) | copy-start | bytes 1179652
  446.1 32.1 %all-to-all-start.2 = ((bf16[2,4,192,768]{3,2,0,1:T(8,128)(2,1)}), bf16[2,4,192,768]{3,2,0,1:T(8,128)(2,1)S(1)}, u32[]{:S(2)}, u32[]{:S(2)}) async-start(bf16[2,4,192,768]{3,2,0,1:T(8,128)(2,1)} %copy.344), calls=%async_computation.2 | async-start | bytes 4718592 | tf_op jit(solution)/shard_map/all_to_all | solution.py:344
  449.7 342.0 %all-reduce.9.cloned.1.call-start = ((), (), s32[]{:S(2)}) async-start(), calls=%async_computation.6 | async-start | bytes 17301504 | tf_op jit(solution)/shard_map/psum | solution.py:387
  478.2 77.2 %all-to-all-start.4 = ((bf16[2,4,192,768]{3,2,0,1:T(8,128)(2,1)}), bf16[2,4,192,768]{3,2,0,1:T(8,128)(2,1)}, u32[]{:S(2)}, u32[]{:S(2)}) async-start(bf16[2,4,192,768]{3,2,0,1:T(8,128)(2,1)} %copy.368), calls=%async_computation.4 | async-start | bytes 4718592 | tf_op jit(solution)/shard_map/all_to_all | solution.py:384
  482.7 434.8 %all-reduce.7.cloned.1.call-start = ((), (), s32[]{:S(2)}) async-start(), calls=%async_computation.5 | async-start | bytes 6291456 | tf_op jit(solution)/shard_map/psum | solution.py:429
  498.5 8.4 copy-start.38
  498.5 8.4 copy-start.39
  714.4 11.4 %copy-start.10 = (f32[12,64,1024]{2,1,0:T(8,128)S(1)}, f32[12,64,1024]{2,1,0:T(8,128)}, u32[]{:S(2)}) copy-start(f32[12,64,1024]{2,1,0:T(8,128)} %fusion.168) | copy-start | bytes 9437188
  730.0 29.7 %copy-start.30 = (bf16[1024,12,64]{0,2,1:T(8,128)(2,1)}, bf16[1024,12,64]{0,2,1:T(8,128)(2,1)S(1)}, u32[]{:S(2)}) copy-start(bf16[1024,12,64]{0,2,1:T(8,128)(2,1)S(1)} %get-tuple-element.148) | copy-start | bytes 4718596
  730.0 30.9 %copy-start.28 = (bf16[1024,12,64]{0,2,1:T(8,128)(2,1)}, bf16[1024,12,64]{0,2,1:T(8,128)(2,1)S(1)}, u32[]{:S(2)}) copy-start(bf16[1024,12,64]{0,2,1:T(8,128)(2,1)S(1)} %get-tuple-element.147) | copy-start | bytes 4718596
  732.6 23.5 %copy-start.7 = (f32[1024,768]{0,1:T(8,128)S(1)}, f32[1024,768]{0,1:T(8,128)}, u32[]{:S(2)}) copy-start(f32[1024,768]{0,1:T(8,128)} %copy-done.6) | copy-start | bytes 9437188
  (88 other events, 277.1 us)
Sparse Core Ops, SparseCore 0:
  471.1 281.4 all-reduce.8
  777.5 139.9 all-reduce.6
where the time goes:
time: 937 us; the launch traced here: 931 us
  matrix products  330 us (35%)
  local copies, waits for them, and re-layouts  217 us (23%)
  other arithmetic  216 us (23%)
  waiting for transfers between devices  129 us (14%)
  starting transfers between devices  21.7 us (2%)
  between operations  17.5 us (2%)
    psum x1, waiting for transfers between devices, body(): lax.psum((jnp.stack([down_query, down_key, down_value, down_output]), jnp...  120 us
    unnamed x273, local copies, waits for them, and re-layouts  43.2 us
    convert_element_type x1, other arithmetic, attend_back(): back_scores = (probabilities * (back_probs - jnp.sum(probabilities * back...  41.9 us
    reduce_sum x1, other arithmetic, body(): back_gates = jnp.sum(back_out[:, None, :] * outputs_all, axis=-1)  40.3 us
    reduce_sum x1, other arithmetic, body(): jnp.sum(back_const * expert_float[:, None, :], axis=-1)  39.2 us
    dot_general x1, matrix products, attend_back(): jnp.einsum('qhd,khd->hqk', back_mixed, values, preferred_element_type=jnp...  35.3 us
    dot_general x1, matrix products, expert_forward(): jnp.einsum('erk,ekf->erf', inner_gate, in_up[:, 0], preferred_element_typ...  29.6 us
    dot_general x1, matrix products, masked_scores(): jnp.einsum('qhd,khd->hqk', queries, key_rows, preferred_element_type=jnp....  22.4 us
  transfers between devices with their start and end apart: 7, of which 3 were waited for; matrix products, arithmetic and copies ran while one was open for 67% of the time, Pallas kernels for 0%

commit v1 on v0

v1 whole, which is shorter than its diff:
```python
import functools
import math

import jax
import jax.numpy as jnp
import numpy as np
from jax import lax
from jax.experimental import pallas as pl
from jax.experimental.pallas import tpu as pltpu
from jax.sharding import PartitionSpec as P

HEADS = 12
HD = 64
EXPERTS = 8
RANK = 16
CAP = 192
EPSILON = 1e-06
F32 = jnp.float32
BF = jnp.bfloat16
NEG = -1e30
LANES = 128
TILE = 256
FTILE = 512
PAIRS = HEADS // 2
META = 8
MIX_ROW = 16
VECTOR_ROW = 20
TARGET_LANE = 24
KEEP_LANE = 26
PIECE = CAP + META


def mm(left, right):
    return jnp.dot(left, right, preferred_element_type=F32)


def mm_nt(left, right):
    return lax.dot_general(left, right, (((1,), (1,)), ((), ())), preferred_element_type=F32)


def mm_tn(left, right):
    return lax.dot_general(left, right, (((0,), (0,)), ((), ())), preferred_element_type=F32)


def iota(shape, axis):
    return lax.broadcasted_iota(jnp.int32, shape, axis)


def hot(condition):
    return jnp.where(condition, 1.0, 0.0).astype(BF)


def split2(value):
    high = value.astype(BF)
    return high, (value - high.astype(F32)).astype(BF)


def split3(value):
    high = value.astype(BF)
    rest = value - high.astype(F32)
    middle = rest.astype(BF)
    return high, middle, (rest - middle.astype(F32)).astype(BF)


def whole(shape):
    zeros = (0,) * len(shape)
    return pl.BlockSpec(shape, lambda *_: zeros)


def smem():
    return pl.BlockSpec(memory_space=pltpu.SMEM)


def tall(width):
    return pl.BlockSpec((TILE, width), lambda i: (i, 0))


def wide(height):
    return pl.BlockSpec((height, TILE), lambda i: (0, i))


def shape_of(*shape, dtype=BF):
    return jax.ShapeDtypeStruct(shape, dtype)


def cost(flops, nbytes, trans=0):
    return pl.CostEstimate(flops=1, bytes_accessed=1, transcendentals=0)


@functools.lru_cache(maxsize=None)
def turn_tables(length_in):
    half = HD // 2
    inverse = np.exp(
        np.arange(half, dtype=np.float32) * np.float32(-2.0 * math.log(10000.0) / HD)
    ).astype(np.float32)
    angles = np.arange(length_in, dtype=np.float32)[:, None] * inverse[None, :]
    cosine = np.tile(np.cos(angles.astype(np.float64)).astype(np.float32), (1, 4))
    sine = np.sin(angles.astype(np.float64)).astype(np.float32)
    return cosine, np.tile(np.concatenate([-sine, sine], axis=1), (1, 2))


def rope(value, cosine, sine):
    first = iota(value.shape, 1) % HD < HD // 2
    turned = jnp.where(first, pltpu.roll(value, LANES - HD // 2, 1), pltpu.roll(value, HD // 2, 1))
    return value * cosine + turned * sine


def find_slots(length, rows_ref, slot_ref):
    tok_count = slot_ref.shape[1]
    before = hot(iota((TILE, TILE), 0) < iota((TILE, TILE), 1))
    carry = jnp.zeros((2 * EXPERTS, 1), F32)
    for start in range(0, tok_count, TILE):
        span = slice(start, start + TILE)
        expert = iota((2 * EXPERTS, TILE), 0).astype(F32)
        token = iota((2 * EXPERTS, TILE), 1) + start
        named = (rows_ref[12:13, span] == expert) | (rows_ref[13:14, span] == expert)
        hit = named & (token < length) & (expert < EXPERTS)
        hits = jnp.where(hit, 1.0, 0.0)
        slots = mm(hits.astype(BF), before) + carry
        carry = carry + jnp.sum(hits, axis=1, keepdims=True)
        slot_ref[:, span] = jnp.where(hit, slots, -1.0)[:EXPERTS].astype(jnp.int32)


def pick_rows(slot_ref, step, me, local):
    first = jnp.bitwise_xor(step, me) * local
    place = iota((CAP, slot_ref.shape[1]), 0)
    return first, [hot(place == slot_ref[pl.ds(first + index, 1), :]) for index in range(local)]


def store_piece(out_refs, step, other, index, value, start):
    @pl.when(step == other)
    def _():
        out_refs[index][start : start + value.shape[0], :] = value


def route_body(local, group, len_ref, me_ref, rows_ref, source_ref, slot_ref, *out_refs):
    step = pl.program_id(0)

    @pl.when(step == 0)
    def _():
        find_slots(len_ref[0], rows_ref, slot_ref)

    _, chosen = pick_rows(slot_ref, step, me_ref[0], local)
    rows = mm(jnp.concatenate(chosen, axis=0), source_ref[...]).astype(BF)
    for other in range(group):
        store_piece(out_refs, step, other, other, rows, 0)


def route_call(local, group, length, me, rows, source):
    tok_count, width = source.shape
    return pl.pallas_call(
        functools.partial(route_body, local, group),
        grid=(group,),
        in_specs=[smem(), smem(), whole(rows.shape), whole(source.shape)],
        out_specs=[whole((EXPERTS, tok_count))] + [whole((local * CAP, width))] * group,
        out_shape=[shape_of(EXPERTS, tok_count, dtype=jnp.int32)]
        + [shape_of(local * CAP, width)] * group,
        cost_estimate=cost(2 * EXPERTS * CAP * tok_count * width, 6e6),
        name="route_rows",
    )(length, me, rows, source)


def send_body(local, group, me_ref, id_ref, slot_ref, data_ref, source_ref, *out_refs):
    step = pl.program_id(0)
    width = source_ref.shape[1]
    first, chosen = pick_rows(slot_ref, step, me_ref[0], local)
    rows = mm(jnp.concatenate(chosen, axis=0), source_ref[...]).astype(BF)
    for index in range(local):
        pieces = split3(data_ref[pl.ds(first + index, 1), :])
        stack = jnp.concatenate(
            [piece.astype(F32) for piece in pieces]
            + [jnp.zeros((13, chosen[index].shape[1]), F32)],
            axis=0,
        ).astype(BF)
        gates = mm_nt(stack, chosen[index])[0:META]
        gates = jnp.where(iota(gates.shape, 0) == 3, id_ref[0].astype(F32), gates)
        meta = jnp.concatenate([gates, jnp.zeros((META, width - CAP), F32)], axis=1)
        kept = rows[index * CAP : index * CAP + CAP]
        for other in range(group):
            far = other >= group // 2
            place = group // 2 + (other - group // 2) * local + index if far else other
            start = 0 if far else index * PIECE
            store_piece(out_refs, step, other, place, kept, start)
            store_piece(out_refs, step, other, place, meta.astype(BF), start + CAP)


def send_call(local, group, me, ids, slots, data, source):
    tok_count, width = source.shape
    heights = [local * PIECE] * (group // 2) + [PIECE] * ((group - group // 2) * local)
    return pl.pallas_call(
        functools.partial(send_body, local, group),
        grid=(group,),
        in_specs=[smem(), smem(), whole(slots.shape), whole(data.shape), whole(source.shape)],
        out_specs=[whole((height, width)) for height in heights],
        out_shape=[shape_of(height, width) for height in heights],
        cost_estimate=cost(2 * EXPERTS * CAP * tok_count * width, 6e6),
        name="send_rows",
    )(me, ids, slots, data, source)


def pre_body(
    id_ref, x_ref, gain_ref, w_ref, ad_ref, au_ref, cos_ref, sin_ref, small_ref, vec_ref,
    normed_ref, inner_ref, q_ref, k_ref, v_ref, acat_ref, bcat_ref, table_ref,
):
    @pl.when(pl.program_id(0) == 0)
    def _():
        first = RANK * id_ref[0]
        total = None
        for index in range(4):
            row, column = iota((LANES, LANES), 0), iota((LANES, LANES), 1)
            place = hot((row >= first) & (row < first + RANK) & (column == (row - first) * 4 + index))
            part = mm(ad_ref[index], place)
            total = part if total is None else total + part
            place = hot(
                (column >= first) & (column < first + RANK) & (row == (column - first) * 4 + index)
            )
            bcat_ref[index] = mm(place, au_ref[index]).astype(BF)
        acat_ref[...] = total.astype(BF)
        table = small_ref[...].T
        number = iota(table.shape, 0)
        for index in range(2):
            table = jnp.where(number == VECTOR_ROW + index, vec_ref[index : index + 1, :], table)
        table_ref[...] = table

    x = x_ref[...].astype(F32)
    scale = lax.rsqrt(jnp.mean(x * x, axis=-1, keepdims=True) + EPSILON)
    normed = (x * scale * gain_ref[0:1, :]).astype(BF)
    normed_ref[...] = normed
    inner = mm(normed, acat_ref[...]).astype(BF)
    inner_ref[...] = inner
    for index, out_ref in enumerate((q_ref, k_ref, v_ref)):
        value = mm(normed, w_ref[index]) + mm(inner, bcat_ref[index])
        if index == 2:
            out_ref[...] = value.astype(BF)
            continue
        for pair in range(PAIRS):
            span = slice(pair * LANES, pair * LANES + LANES)
            turned = rope(value[:, span], cos_ref[...], sin_ref[...]).astype(BF)
            if index == 0:
                turned = (turned.astype(F32) * HD**-0.5).astype(BF)
            out_ref[:, span] = turned


def pre_call(ids, tokens, gains, weights, down, upper, cosine, sine, small, vectors):
    tok_count, width = tokens.shape
    return pl.pallas_call(
        pre_body,
        grid=(tok_count // TILE,),
        in_specs=[
            smem(), tall(width), whole(gains.shape), whole(weights.shape), whole(down.shape),
            whole(upper.shape), tall(LANES), tall(LANES), whole(small.shape), whole(vectors.shape),
        ],
        out_specs=[
            tall(width), tall(LANES), tall(width), tall(width), tall(width),
            whole((width, LANES)), whole(upper.shape), whole((LANES, width)),
        ],
        out_shape=[
            shape_of(tok_count, width), shape_of(tok_count, LANES), shape_of(tok_count, width),
            shape_of(tok_count, width), shape_of(tok_count, width), shape_of(width, LANES),
            shape_of(*upper.shape), shape_of(LANES, width, dtype=F32),
        ],
        cost_estimate=cost(2 * tok_count * width * width * 3.5, 14e6),
        name="before_attention",
    )(ids, tokens, gains, weights, down, upper, cosine, sine, small, vectors)


def attend_body(len_ref, q_ref, k_ref, v_ref, mixed_ref, q2_ref):
    tok_count = q_ref.shape[0]
    lane = iota((tok_count, LANES), 1)
    position = iota((tok_count, LANES), 0)
    bias = jnp.where(position < len_ref[0], 0.0, NEG)
    causal = iota((TILE, TILE), 1) <= iota((TILE, TILE), 0)
    lane_tile = lane[:TILE]
    outs = [[], []]
    for head in range(2):
        own = lane // HD == head
        spare = HD * (1 - head)
        one = jnp.where(lane == spare, 1.0, 0.0)
        queries = jnp.where(own, q_ref[...].astype(F32), one)
        keys = jnp.where(
            own, k_ref[...].astype(F32), jnp.where(lane == spare, bias, 0.0)
        ).astype(BF)
        values = jnp.where(own, v_ref[...].astype(F32), one).astype(BF)
        for start in range(0, tok_count, TILE):
            stop = start + TILE
            part = queries[start:stop]
            scores = mm_nt(part.astype(BF), keys[:stop])
            diagonal = jnp.where(causal, scores[:, start:], NEG)
            scores = diagonal if start == 0 else jnp.concatenate([scores[:, :start], diagonal], axis=1)
            top = jnp.max(scores, axis=-1, keepdims=True)
            weights = jnp.exp(scores - top).astype(BF)
            mixed = mm(weights, values[:stop])
            total = mixed[:, spare : spare + 1]
            outs[head].append(mixed / total)
            log_total = top + jnp.log(total)
            high, middle, low = split3(log_total)
            kept = part
            for offset, piece in enumerate((high, middle, low)):
                kept = jnp.where(lane_tile == spare + 1 + offset, piece.astype(F32), kept)
            q2_ref[start:stop, head * LANES : head * LANES + LANES] = kept.astype(BF)
    for index, start in enumerate(range(0, tok_count, TILE)):
        mixed_ref[start : start + TILE, :] = jnp.where(
            lane_tile < HD, outs[0][index], outs[1][index]
        ).astype(BF)


def attend_call(length, queries, keys, values):
    tok_count, width = queries.shape
    column = pl.BlockSpec((tok_count, LANES), lambda i: (0, i))
    return pl.pallas_call(
        attend_body,
        grid=(PAIRS,),
        in_specs=[smem(), column, column, column],
        out_specs=[column, pl.BlockSpec((tok_count, 2 * LANES), lambda i: (0, i))],
        out_shape=[shape_of(tok_count, width), shape_of(tok_count, 2 * width)],
        cost_estimate=cost(
            2.5 * tok_count * tok_count * width, 9e6, 0.6 * HEADS * tok_count * tok_count
        ),
        name="attention_forward",
    )(length, queries, keys, values)


def attend_back_body(
    len_ref, q2_ref, k_ref, v_ref, mixed_ref, back_ref, cos_ref, sin_ref,
    dq_ref, dk_ref, dv_ref, acc_ref,
):
    tok_count = k_ref.shape[0]
    lane = iota((tok_count, LANES), 1)
    position = iota((tok_count, LANES), 0)
    bias = jnp.where(position < len_ref[0], 0.0, NEG)
    causal = iota((TILE, TILE), 0) <= iota((TILE, TILE), 1)
    back = back_ref[...].astype(F32)
    product = back * mixed_ref[...].astype(F32)
    grads = []
    for head in range(2):
        own = lane // HD == head
        spare = HD * (1 - head)
        minus = jnp.where((lane > spare) & (lane < spare + 4), -1.0, 0.0)
        q2 = q2_ref[:, head * LANES : head * LANES + LANES]
        k2f = jnp.where(
            own, k_ref[...].astype(F32), jnp.where(lane == spare, bias, minus)
        )
        k2 = k2f.astype(BF)
        k2t = k2f.T.astype(BF)
        v2 = jnp.where(own, v_ref[...].astype(F32), minus).astype(BF)
        delta = jnp.sum(jnp.where(own, product, 0.0), axis=-1, keepdims=True)
        back2 = jnp.where(own, back, 0.0)
        for offset, piece in enumerate(split3(delta)):
            back2 = jnp.where(lane == spare + 1 + offset, piece.astype(F32), back2)
        back2 = back2.astype(BF)
        dk_parts, dv_parts = [], []
        for start in range(0, tok_count, TILE):
            stop = start + TILE
            scores = mm_nt(k2[start:stop], q2[start:])
            slopes = mm_nt(v2[start:stop], back2[start:])
            diagonal = jnp.where(causal, scores[:, :TILE], NEG)
            scores = (
                diagonal
                if stop == tok_count
                else jnp.concatenate([diagonal, scores[:, TILE:]], axis=1)
            )
            weights = jnp.exp(scores)
            turned = (weights * slopes).astype(BF)
            dv_parts.append(mm(weights.astype(BF), back2[start:]))
            dk_parts.append(mm(turned, q2[start:]))
            update = mm(k2t[:, start:stop], turned)
            if start == 0:
                acc_ref[head] = update
            else:
                acc_ref[head, :, start:] += update
        grads.append((jnp.concatenate(dk_parts, axis=0), jnp.concatenate(dv_parts, axis=0)))
    low_lane = lane < HD
    cosine, sine = cos_ref[...], -sin_ref[...]
    row = iota((LANES, tok_count), 0)
    dq = jnp.where(row < HD, acc_ref[0], acc_ref[1]).T * HD**-0.5
    dq_ref[...] = rope(dq, cosine, sine).astype(BF)
    dk = jnp.where(low_lane, grads[0][0], grads[1][0])
    dk_ref[...] = rope(dk, cosine, sine).astype(BF)
    dv_ref[...] = jnp.where(low_lane, grads[0][1], grads[1][1]).astype(BF)


def attend_back_call(length, q2, keys, values, mixed, back, cosine, sine):
    tok_count, width = keys.shape
    column = pl.BlockSpec((tok_count, LANES), lambda i: (0, i))
    return pl.pallas_call(
        attend_back_body,
        grid=(PAIRS,),
        in_specs=[
            smem(), pl.BlockSpec((tok_count, 2 * LANES), lambda i: (0, i)), column, column, column,
            column, whole(cosine.shape), whole(sine.shape),
        ],
        out_specs=[column] * 3,
        out_shape=[shape_of(tok_count, width)] * 3,
        scratch_shapes=[pltpu.VMEM((2, LANES, tok_count), F32)],
        cost_estimate=cost(
            6 * tok_count * tok_count * width, 14e6, 0.6 * HEADS * tok_count * tok_count
        ),
        name="attention_backward",
    )(length, q2, keys, values, mixed, back, cosine, sine)


def post_body(
    local, group, me_ref, mixed_ref, x_ref, wo_ref, acat_ref, bcat_ref, gain_ref, table_ref, mix_ref,
    rows_ref, slot_ref, hidden_ref, ei_ref, inner_ref, data_ref, cols_ref,
):
    mixed = mixed_ref[...]
    inner = mm(mixed, acat_ref[...]).astype(BF)
    inner_ref[...] = inner
    hidden = x_ref[...].astype(F32) + (mm(mixed, wo_ref[...]) + mm(inner, bcat_ref[0]))
    hidden_ref[...] = hidden
    scale = lax.rsqrt(jnp.mean(hidden * hidden, axis=-1, keepdims=True) + EPSILON)
    ei = (hidden * scale * gain_ref[1:2, :]).astype(BF)
    ei_ref[...] = ei
    read = None
    for piece in split3(table_ref[...]):
        part = mm_nt(piece, ei)
        read = part if read is None else read + part
    logits = read[0:16]
    for index in range(EXPERTS + 4):
        logits = logits + mix_ref[:, index : index + 1] * rows_ref[index : index + 1, :]
    first, second = rows_ref[12:13, :], rows_ref[13:14, :]
    number = iota((16, TILE), 0).astype(F32)
    one = jnp.sum(jnp.where(number == first, logits, 0.0), axis=0, keepdims=True)
    two = jnp.sum(jnp.where(number == second, logits, 0.0), axis=0, keepdims=True)
    top = jnp.maximum(one, two)
    one, two = jnp.exp(one - top), jnp.exp(two - top)
    gate_a, gate_b = one / (one + two), two / (one + two)
    mixes = read[MIX_ROW : MIX_ROW + 4]
    shares = []
    for index in range(2):
        left, right = mixes[2 * index : 2 * index + 1], mixes[2 * index + 1 : 2 * index + 2]
        top = jnp.maximum(left, right)
        left, right = jnp.exp(left - top), jnp.exp(right - top)
        shares += [left / (left + right), right / (left + right)]

    def both(value):
        return jnp.where(first == value, gate_a, 0.0) + jnp.where(second == value, gate_b, 0.0)

    gates = jnp.where(number == first, gate_a, 0.0) + jnp.where(number == second, gate_b, 0.0)
    beta_a, beta_b = both(EXPERTS + 2.0), both(EXPERTS + 3.0)
    keep = both(EXPERTS + 1.0) + beta_a * shares[0] + beta_b * shares[2]
    data_ref[0:8, :] = gates[0:8]
    tail = [gate_a, gate_b] + shares + [beta_a, beta_b]
    data_ref[8:16, :] = jnp.concatenate(tail, axis=0)
    slots = slot_ref[...].astype(F32)
    expert = iota((EXPERTS, TILE), 0)
    partner = jnp.bitwise_xor(expert // local, me_ref[0])
    base = ((expert % local) * (group * CAP) + partner * CAP).astype(F32)
    place = jnp.where(slots >= 0, slots + base + 1.0, 0.0)
    expert = expert.astype(F32)
    target_a = jnp.sum(jnp.where(expert == first, place, 0.0), axis=0, keepdims=True) - 1.0
    target_b = jnp.sum(jnp.where(expert == second, place, 0.0), axis=0, keepdims=True) - 1.0
    stack = jnp.concatenate(
        [jnp.zeros((VECTOR_ROW, TILE), F32), beta_a * shares[1], beta_b * shares[3]]
        + [jnp.zeros((2, TILE), F32), target_a, target_b, keep]
        + [jnp.zeros((LANES - KEEP_LANE - 1, TILE), F32)],
        axis=0,
    )
    cols_ref[...] = stack.T


def post_call(
    local, group, me, mixed, tokens, weight, acat, bcat, gains, table, mixer, rows, slots
):
    tok_count, width = tokens.shape
    return pl.pallas_call(
        functools.partial(post_body, local, group),
        grid=(tok_count // TILE,),
        in_specs=[
            smem(), tall(width), tall(width), whole(weight.shape), whole(acat.shape),
            pl.BlockSpec((1, LANES, width), lambda i: (3, 0, 0)), whole(gains.shape),
            whole(table.shape), whole(mixer.shape), wide(16), wide(EXPERTS),
        ],
        out_specs=[tall(width), tall(width), tall(LANES), wide(16), tall(LANES)],
        out_shape=[
            shape_of(tok_count, width, dtype=F32), shape_of(tok_count, width),
            shape_of(tok_count, LANES), shape_of(16, tok_count, dtype=F32),
            shape_of(tok_count, LANES, dtype=F32),
        ],
        cost_estimate=cost(2 * tok_count * width * width * 1.5, 11e6),
        name="after_attention",
    )(me, mixed, tokens, weight, acat, bcat, gains, table, mixer, rows, slots)


def expert_body(
    pair, per_owner, group, steps, has_grad, *refs
):
    count = len(pair)
    piece_refs, refs = refs[:count], refs[count:]
    cot_refs, refs = refs[:count], refs[count:]
    wg_ref, wu_ref, wd_ref, dn_ref, up_ref, od_ref, ou_ref = refs[:7]
    refs = refs[7:]
    before_ref = None
    if has_grad:
        before_ref, refs = refs[0], refs[1:]
    back_refs, refs = refs[:count], refs[count:]
    out_refs, refs = refs[:count], refs[count:]
    (
        grad_ref, x_ref, g_ref, gate_ref, pick_ref, dr_ref, zg_ref, zu_ref, dzd_ref, zgt_ref, zut_ref,
        dzdt_ref, racc_ref, xacc_ref, zd_acc, dzg_acc, dzu_acc, h_ref, dg_ref, du_ref,
    ) = refs
    step = pl.program_id(0)
    rows, width = x_ref.shape
    compact = group * RANK
    chosen = pick_ref[...] > 0.0

    def fold(value):
        place = iota((compact, LANES), 0)
        block = per_owner * group
        inner = place // block * per_owner + place % per_owner
        folded = mm_nt(hot(iota((compact, LANES), 1) % RANK == inner), value)
        place = iota((compact, rows), 0)
        owner = place % block // per_owner
        mine = iota((compact, rows), 1) // CAP + pair[0]
        return jnp.where(mine == owner, folded, 0.0).astype(BF)

    def put(start, value):
        span = pl.ds(start, value.shape[1])
        if has_grad:
            value = value + before_ref[:, span].astype(F32)
        grad_ref[:, span] = value.astype(BF)

    @pl.when(step == 0)
    def _():
        for index in range(count):
            span = slice(index * CAP, index * CAP + CAP)
            x_ref[span] = piece_refs[index][0:CAP]
            g_ref[span] = cot_refs[index][...]
            meta = piece_refs[index][CAP:PIECE].astype(F32)
            gate = (meta[0:1] + meta[1:2] + meta[2:3])[:, 0 : 2 * LANES]
            gate_ref[span] = jnp.broadcast_to(gate, (LANES, 2 * LANES)).T[0:CAP]
            lane = (iota((CAP, LANES), 1) // RANK).astype(F32)
            pick_ref[span] = jnp.where(lane == meta[3:4, 0:LANES], 1.0, 0.0)
        picked = pick_ref[...] > 0.0
        dr = (gate_ref[:, 0:1] * g_ref[...].astype(F32)).astype(BF)
        dr_ref[...] = dr
        zg = jnp.where(picked, mm(x_ref[...], dn_ref[0]), 0.0).astype(BF)
        zu = jnp.where(picked, mm(x_ref[...], dn_ref[1]), 0.0).astype(BF)
        dzd = jnp.where(picked, mm_nt(dr, ou_ref[...]), 0.0).astype(BF)
        zg_ref[...] = zg
        zu_ref[...] = zu
        dzd_ref[...] = dzd
        zgt_ref[...] = fold(zg)
        zut_ref[...] = fold(zu)
        dzdt_ref[...] = fold(dzd)
        for ref in (racc_ref, xacc_ref, zd_acc, dzg_acc, dzu_acc):
            ref[...] = jnp.zeros_like(ref)

    gate = mm(x_ref[...], wg_ref[...]) + mm(zg_ref[...], up_ref[0])
    upper = mm(x_ref[...], wu_ref[...]) + mm(zu_ref[...], up_ref[1])
    share = 0.5 * jnp.tanh(0.5 * gate) + 0.5
    silu = gate * share
    active = (silu * upper).astype(BF)
    h_ref[...] = active
    back = mm_nt(dr_ref[...], wd_ref[...]) + mm_nt(dzd_ref[...], od_ref[...])
    du = (back * silu).astype(BF)
    dg = (back * upper * (share + silu * (1.0 - share))).astype(BF)
    du_ref[...] = du
    dg_ref[...] = dg
    racc_ref[...] += mm(active, wd_ref[...])
    zd_acc[...] += mm(active, od_ref[...])
    xacc_ref[...] += mm_nt(dg, wg_ref[...]) + mm_nt(du, wu_ref[...])
    dzg_acc[...] += mm_nt(dg, up_ref[0])
    dzu_acc[...] += mm_nt(du, up_ref[1])
    tile = h_ref.shape[1]
    total = steps * tile
    at = pl.multiple_of(step * tile, tile)
    put(at, mm(zgt_ref[...], dg_ref[...]))
    put(total + at, mm(zut_ref[...], du_ref[...]))
    put(2 * total + at, mm(dzdt_ref[...], h_ref[...]))

    @pl.when(step == steps - 1)
    def _():
        zd = jnp.where(chosen, zd_acc[...], 0.0).astype(BF)
        dzg = jnp.where(chosen, dzg_acc[...], 0.0).astype(BF)
        dzu = jnp.where(chosen, dzu_acc[...], 0.0).astype(BF)
        result = racc_ref[...] + mm(zd, ou_ref[...])
        gated = (gate_ref[:, 0:1] * result).astype(BF)
        product = g_ref[...].astype(F32) * result.astype(BF).astype(F32)
        dots = jnp.broadcast_to(jnp.sum(product, axis=-1, keepdims=True), (rows, LANES))
        back_rows = (xacc_ref[...] + mm_nt(dzg, dn_ref[0]) + mm_nt(dzu, dn_ref[1])).astype(BF)
        for index in range(count):
            span = slice(index * CAP, index * CAP + CAP)
            out_refs[index][...] = gated[span]
            back_refs[index][0:CAP, :] = back_rows[span]
            column = jnp.concatenate(
                [dots[span], jnp.zeros((2 * LANES - CAP, LANES), F32)], axis=0
            ).T[0:1]
            meta = jnp.concatenate(
                [piece.astype(F32) for piece in split3(column)]
                + [jnp.zeros((META - 3, 2 * LANES), F32)],
                axis=0,
            )
            meta = jnp.concatenate([meta, jnp.zeros((META, width - 2 * LANES), F32)], axis=1)
            back_refs[index][CAP:PIECE, :] = meta.astype(BF)
        base = 3 * total
        put(base, mm(fold(zd), dr_ref[...]))
        put(base + width, mm(fold(dzg), x_ref[...]))
        put(base + 2 * width, mm(fold(dzu), x_ref[...]))


def expert_call(index, pair, group, per_owner, pieces, cots, before, weights):
    gate_w, up_w, down_w, in_down, in_up, out_down, out_up = weights
    width, hidden = gate_w.shape[1:]
    rows = len(pair) * CAP
    steps = hidden // FTILE
    columns = 3 * hidden + 3 * width
    compact = group * RANK
    has_grad = before is not None
    return pl.pallas_call(
        functools.partial(expert_body, pair, per_owner, group, steps, has_grad),
        grid=(steps,),
        in_specs=[
            pl.BlockSpec((PIECE, width), lambda f, row=piece.shape[0] // PIECE > 1: (index * row, 0))
            for piece in pieces
        ]
        + [pl.BlockSpec((CAP, width), lambda f: (index, 0))] * len(pair)
        + [
            pl.BlockSpec((None, width, FTILE), lambda f: (index, 0, f)),
            pl.BlockSpec((None, width, FTILE), lambda f: (index, 0, f)),
            pl.BlockSpec((None, FTILE, width), lambda f: (index, f, 0)),
            pl.BlockSpec((None, 2, width, LANES), lambda f: (index, 0, 0, 0)),
            pl.BlockSpec((None, 2, LANES, FTILE), lambda f: (index, 0, 0, f)),
            pl.BlockSpec((None, FTILE, LANES), lambda f: (index, f, 0)),
            pl.BlockSpec((None, LANES, width), lambda f: (index, 0, 0)),
        ]
        + [whole((compact, columns))] * has_grad,
        out_specs=[whole((PIECE, width))] * len(pair)
        + [whole((CAP, width))] * len(pair)
        + [whole((compact, columns))],
        out_shape=[shape_of(PIECE, width)] * len(pair)
        + [shape_of(CAP, width)] * len(pair)
        + [shape_of(compact, columns)],
        scratch_shapes=[pltpu.VMEM((rows, width), BF)] * 2
        + [pltpu.VMEM((rows, LANES), F32)] * 2
        + [pltpu.VMEM((rows, width), BF)]
        + [pltpu.VMEM((rows, LANES), BF)] * 3
        + [pltpu.VMEM((compact, rows), BF)] * 3
        + [pltpu.VMEM((rows, width), F32)] * 2
        + [pltpu.VMEM((rows, LANES), F32)] * 3
        + [pltpu.VMEM((rows, FTILE), BF)] * 3,
        cost_estimate=cost(2 * rows * width * hidden * 8, 16e6, rows * hidden),
        name="expert_layer",
    )(
        *pieces, *cots, gate_w, up_w, down_w, in_down, in_up, out_down, out_up,
        *([before] if has_grad else []),
    )


def spread(cols_ref, index, count):
    return iota((TILE, count), 1).astype(F32) == cols_ref[:, index : index + 1]


def combine_body(
    pieces, len_ref, *refs
):
    back_refs = refs[:pieces]
    (
        rows_ref, data_ref, cols_ref, cot_ref, ei_ref, hidden_ref, gain_ref, wo_ref, acat_ref, bcat_ref,
        table_ref, bh_ref, ba_ref, din_ref, bm_ref, back_all, dots_ref,
    ) = refs[pieces:]
    count = pieces * CAP

    @pl.when(pl.program_id(0) == 0)
    def _():
        for index, back_ref in enumerate(back_refs):
            back_all[index * CAP : index * CAP + CAP, :] = back_ref[0:CAP, :]
        dots = [back_ref[CAP:PIECE, 0:CAP].astype(F32) for back_ref in back_refs]
        dots = jnp.concatenate(dots, axis=1)
        dots_ref[...] = jnp.concatenate([dots, jnp.zeros_like(dots)], axis=0).astype(BF)

    chosen_a = hot(spread(cols_ref, TARGET_LANE, count))
    chosen_b = hot(spread(cols_ref, TARGET_LANE + 1, count))
    stack = dots_ref[...]
    routed_a = jnp.sum(mm_nt(stack, chosen_a)[0:8], axis=0, keepdims=True)
    routed_b = jnp.sum(mm_nt(stack, chosen_b)[0:8], axis=0, keepdims=True)
    cot = cot_ref[...]
    cot_f = cot.astype(F32)
    high, low = split2(cot_f * ei_ref[...].astype(F32))
    ones = jnp.ones((16, cot.shape[1]), BF)
    along_x = (mm_nt(ones, high) + mm_nt(ones, low))[0:1]
    table_high, table_middle, table_low = split3(table_ref[...])
    along_c = mm_nt(table_high, cot) + mm_nt(table_middle, cot) + mm_nt(table_low, cot)
    along_a = along_c[VECTOR_ROW : VECTOR_ROW + 1]
    along_b = along_c[VECTOR_ROW + 1 : VECTOR_ROW + 2]
    first, second = rows_ref[12:13, :], rows_ref[13:14, :]
    token = iota((1, TILE), 1) + pl.program_id(0) * TILE
    valid = jnp.where(token < len_ref[0], 1.0, 0.0)
    gate_a, gate_b = data_ref[8:9, :], data_ref[9:10, :]
    share = [data_ref[index : index + 1, :] for index in range(10, 14)]
    beta_a, beta_b = data_ref[14:15, :], data_ref[15:16, :]
    const_a = share[0] * along_x + share[1] * along_a
    const_b = share[2] * along_x + share[3] * along_b

    def here(route):
        return (
            jnp.where(route == EXPERTS + 1.0, along_x, 0.0)
            + jnp.where(route == EXPERTS + 2.0, const_a, 0.0)
            + jnp.where(route == EXPERTS + 3.0, const_b, 0.0)
        )

    dot_a, dot_b = routed_a + here(first), routed_b + here(second)
    mean = gate_a * dot_a + gate_b * dot_b
    chosen_grad_a = valid * gate_a * (dot_a - mean)
    chosen_grad_b = valid * gate_b * (dot_b - mean)
    number = iota((16, TILE), 0).astype(F32)
    logit_grads = jnp.where(number == first, chosen_grad_a, 0.0) + jnp.where(
        number == second, chosen_grad_b, 0.0
    )
    mixes = []
    for index, (beta, along) in enumerate(((beta_a, along_a), (beta_b, along_b))):
        left, right = share[2 * index], share[2 * index + 1]
        weighted = left * along_x + right * along
        mixes += [
            valid * beta * left * (along_x - weighted),
            valid * beta * right * (along - weighted),
        ]
    stack = jnp.concatenate(
        [logit_grads] + mixes + [jnp.zeros((LANES - 20, TILE), F32)], axis=0
    ).T
    high, low = split2(stack)
    inside = iota((TILE, 1), 0) + pl.program_id(0) * TILE < len_ref[0]
    grad = jnp.where(inside, cot_f, 0.0)
    back = mm(high, table_high) + mm(low, table_high) + mm(high, table_middle)
    back = back + cols_ref[:, KEEP_LANE : KEEP_LANE + 1] * grad
    back = back + mm(chosen_a + chosen_b, back_all[...])
    hidden = hidden_ref[...]
    scale = lax.rsqrt(jnp.mean(hidden * hidden, axis=-1, keepdims=True) + EPSILON)
    normed = hidden * scale
    back = back * gain_ref[1:2, :]
    back = grad + scale * (back - normed * jnp.mean(back * normed, axis=-1, keepdims=True))
    bh_ref[...] = back
    rounded = back.astype(BF)
    ba_ref[...] = rounded
    inner = mm_nt(rounded, bcat_ref[0]).astype(BF)
    din_ref[...] = inner
    bm_ref[...] = (mm_nt(rounded, wo_ref[...]) + mm_nt(inner, acat_ref[...])).astype(BF)


def combine_call(
    length, backs, rows, data, cols, cotangent, ei, hidden, gains, weight, acat, bcat, table
):
    tok_count, width = cotangent.shape
    pieces = len(backs)
    return pl.pallas_call(
        functools.partial(combine_body, pieces),
        grid=(tok_count // TILE,),
        in_specs=[smem()] + [whole(back.shape) for back in backs] + [
            wide(16), wide(16), tall(LANES), tall(width), tall(width), tall(width),
            whole(gains.shape), whole(weight.shape), whole(acat.shape),
            pl.BlockSpec((1, LANES, width), lambda i: (3, 0, 0)), whole(table.shape),
        ],
        out_specs=[tall(width), tall(width), tall(LANES), tall(width)],
        out_shape=[
            shape_of(tok_count, width, dtype=F32), shape_of(tok_count, width),
            shape_of(tok_count, LANES), shape_of(tok_count, width),
        ],
        scratch_shapes=[
            pltpu.VMEM((pieces * CAP, width), BF), pltpu.VMEM((2 * META, pieces * CAP), BF)
        ],
        cost_estimate=cost(2 * tok_count * width * width * 4, 18e6),
        name="combine_backward",
    )(
        length, *backs, rows, data, cols, cotangent, ei, hidden, gains, weight, acat, bcat, table
    )


def result_body(pieces, len_ref, *refs):
    result_refs = refs[:pieces]
    cols_ref, ei_ref, hidden_ref, table_ref, out_ref, result_all = refs[pieces:]
    count = pieces * CAP

    @pl.when(pl.program_id(0) == 0)
    def _():
        for index, result_ref in enumerate(result_refs):
            result_all[index * CAP : index * CAP + CAP, :] = result_ref[...]

    both = hot(
        spread(cols_ref, TARGET_LANE, count) | spread(cols_ref, TARGET_LANE + 1, count)
    )
    cols = cols_ref[...]
    high, low = split2(cols)
    table_high, table_low = split2(table_ref[...])
    mixture = mm(high, table_high) + mm(low, table_high) + mm(high, table_low)
    mixture = mixture + cols[:, KEEP_LANE : KEEP_LANE + 1] * ei_ref[...].astype(F32)
    mixture = mixture + mm(both, result_all[...])
    inside = iota((TILE, 1), 0) + pl.program_id(0) * TILE < len_ref[0]
    out_ref[...] = (hidden_ref[...] + jnp.where(inside, mixture, 0.0)).astype(BF)


def result_call(length, results, cols, ei, hidden, table):
    tok_count, width = ei.shape
    pieces = len(results)
    return pl.pallas_call(
        functools.partial(result_body, pieces),
        grid=(tok_count // TILE,),
        in_specs=[smem()] + [whole(result.shape) for result in results] + [
            tall(LANES), tall(width), tall(width), whole(table.shape),
        ],
        out_specs=tall(width),
        out_shape=shape_of(tok_count, width),
        scratch_shapes=[pltpu.VMEM((pieces * CAP, width), BF)],
        cost_estimate=cost(2 * tok_count * width * width * 2, 10e6),
        name="layer_output",
    )(length, *results, cols, ei, hidden, table)


def last_body(
    packed, dq_ref, dk_ref, dv_ref, w_ref, acat_ref, bcat_ref, normed_ref, inner_ref, mixed_ref, inner_o_ref,
    ba_ref, din_ref, x_ref, bh_ref, gain_ref, out_ref, grad_ref, acc_ref,
):
    step = pl.program_id(0)
    width = x_ref.shape[1]
    count = 4 * RANK

    @pl.when(step == 0)
    def _():
        acc_ref[...] = jnp.zeros_like(acc_ref)

    total = None
    inner_t = inner_ref[...].astype(F32).T[0:count].astype(BF)
    outer_t = inner_o_ref[...].astype(F32).T[0:count].astype(BF)
    number = iota((count, width), 0) % 4
    upper = mm(outer_t, ba_ref[...])
    back_inner = din_ref[...].astype(F32)
    for index, ref in enumerate((dq_ref, dk_ref, dv_ref)):
        value = ref[...]
        part = mm_nt(value, w_ref[index])
        total = part if total is None else total + part
        back_inner = back_inner + mm_nt(value, bcat_ref[index]).astype(BF).astype(F32)
        upper = jnp.where(number == index, mm(inner_t, value), upper)
    own = iota(back_inner.shape, 1) % 4 < 3
    total = total + mm_nt(jnp.where(own, back_inner, 0.0).astype(BF), acat_ref[...])
    back_t = back_inner.T[0:count].astype(BF)
    down = jnp.where(number < 3, mm(back_t, normed_ref[...]), mm(back_t, mixed_ref[...]))
    acc_ref[:, 0:width] += down
    acc_ref[:, width:] += upper
    x = x_ref[...].astype(F32)
    scale = lax.rsqrt(jnp.mean(x * x, axis=-1, keepdims=True) + EPSILON)
    normed = x * scale
    back = total * gain_ref[0:1, :]
    back = scale * (back - normed * jnp.mean(back * normed, axis=-1, keepdims=True))
    out_ref[...] = (bh_ref[...] + back).astype(BF)

    @pl.when(step == pl.num_programs(0) - 1)
    def _():
        if not packed:
            grad_ref[...] = acc_ref[...].astype(BF)
            return
        half = width // 2
        shape = (16 * RANK, count)
        place, row = iota(shape, 0), iota(shape, 1)
        total = None
        for index in range(4):
            kind, part = index // 2, index % 2
            here = (place % 4 == row % 4) & (place // 16 == row // 4)
            here = here & (place // 8 % 2 == part) & (place // 4 % 2 == kind)
            start = kind * width + part * half
            piece = mm(hot(here), acc_ref[:, start : start + half].astype(BF))
            total = piece if total is None else total + piece
        grad_ref[...] = total.astype(BF)


def last_call(
    packed, dq, dk, dv, weights, acat, bcat, normed, inner, mixed, inner_o, ba, din, tokens, bh, gains
):
    tok_count, width = tokens.shape
    grad_shape = (16 * RANK, width // 2) if packed else (4 * RANK, 2 * width)
    return pl.pallas_call(
        functools.partial(last_body, packed),
        grid=(tok_count // TILE,),
        in_specs=[
            tall(width), tall(width), tall(width), whole(weights.shape), whole(acat.shape),
            whole(bcat.shape), tall(width), tall(LANES), tall(width), tall(LANES), tall(width),
            tall(LANES), tall(width), tall(width), whole(gains.shape),
        ],
        out_specs=[tall(width), whole(grad_shape)],
        out_shape=[shape_of(tok_count, width), shape_of(*grad_shape)],
        scratch_shapes=[pltpu.VMEM((4 * RANK, 2 * width), F32)],
        cost_estimate=cost(2 * tok_count * width * width * 4.5, 20e6),
        name="after_attention_backward",
    )(
        dq, dk, dv, weights, acat, bcat, normed, inner, mixed, inner_o, ba, din, tokens, bh, gains
    )


def exchange(value, axes):
    return lax.all_to_all(value, axes, split_axis=0, concat_axis=0, tiled=True)


def gather_all(value, axes, count):
    return exchange(jnp.broadcast_to(value[None], (count,) + value.shape), axes)


def swap(value, partner, group):
    if partner == 0:
        return value
    return lax.ppermute(value, "expert", [(index, index ^ partner) for index in range(group)])


def sum_expert_body(each, group, adapters, me_ref, id_ref, in_ref, out_ref):
    count = in_ref.shape[0]
    column = iota((1, count), 1)
    found = jnp.zeros((1, count), jnp.int32)
    for source in range(count // each):
        device = source // group * group + jnp.bitwise_xor(source % group, me_ref[0])
        found = jnp.where(column // each == source, id_ref[device], found)
    place = iota((adapters * each, count), 0)
    column = iota((adapters * each, count), 1)
    pick = hot((place // each == found) & (place % each == column % each))
    out_ref[...] = mm(pick, in_ref[...]).astype(BF)


def exchange_expert_grads(grads, group, owners):
    split = min(RANK, owners)
    each, parts = RANK // split, owners // split
    columns = grads.shape[1] // parts
    pieces = grads.reshape(split, each * group, parts, columns)
    pieces = pieces.transpose(0, 2, 1, 3).reshape(owners, group * each, columns)
    return exchange(pieces, "dp").reshape(owners * group * each, columns)


def sum_expert_grads(got, me, ids, adapters, group, owners):
    columns = got.shape[1]
    each = RANK // min(RANK, owners)
    return pl.pallas_call(
        functools.partial(sum_expert_body, each, group, adapters),
        in_specs=[smem(), smem(), pl.BlockSpec(memory_space=pltpu.VMEM)],
        out_shape=shape_of(adapters * each, columns),
        cost_estimate=cost(1e9, 5e6),
        name="expert_gradient_part",
    )(me, ids, got)


def finish_expert_body(split, adapters, hidden, in_ref, *refs):
    down_ref, up_ref, out_down_ref, out_up_ref = refs[-4:]
    each = RANK // split
    rows = adapters * each
    count = split * rows
    width = out_up_ref.shape[1]

    def place(value):
        return value // each % adapters * RANK + value // (adapters * each) * each + value % each

    move = hot(iota((count, count), 0) == place(iota((count, count), 1)))
    back = hot(iota((count, count), 1) == place(iota((count, count), 0)))

    def part(start, size):
        span = slice(start, start + size)
        rows_of = [in_ref[owner, :, span] for owner in range(split)]
        return jnp.concatenate(rows_of, axis=0)

    for index in range(2):
        up_ref[index] = mm(move, part(index * hidden, hidden))
    out_down_ref[...] = mm_tn(part(2 * hidden, hidden), back)
    base = 3 * hidden
    out_up_ref[...] = mm(move, part(base, width))
    for index in range(2):
        base += width
        down_ref[index] = mm_tn(part(base, width), back)


def finish_expert_call(owned, adapters, owners, width, hidden):
    local = len(owned)
    rows, columns = owned[0].shape
    everything = [lax.all_gather(own, "dp", axis=0, tiled=False) for own in owned]
    total = adapters * RANK
    shapes = [(local, 2, width, total), (local, 2, total, hidden), (local, hidden, total),
              (local, total, width)]
    outs = []
    for index, value in enumerate(everything):
        specs = [
            pl.BlockSpec((None,) + shape[1:], lambda *_, rank=len(shape): (index,) + (0,) * (rank - 1))
            for shape in shapes
        ]
        outs = pl.pallas_call(
            functools.partial(finish_expert_body, owners, adapters, hidden),
            grid=(1,),
            in_specs=[whole((owners, rows, columns))] + [pl.BlockSpec(memory_space=pl.ANY)] * len(outs),
            out_specs=specs,
            out_shape=[shape_of(*shape, dtype=F32) for shape in shapes],
            input_output_aliases={1 + place: place for place in range(len(outs))},
            cost_estimate=cost(1e9, 8e6),
            name="expert_gradient_sums",
        )(value, *outs)
    return outs


def spread_expert_grads(own, adapters, owners):
    split = min(RANK, owners)
    each, parts = RANK // split, owners // split
    everything = gather_all(own, "dp", owners)
    everything = everything.reshape(split, parts, adapters, each, own.shape[1])
    everything = everything.transpose(2, 0, 3, 1, 4)
    return everything.reshape(adapters * RANK, parts * own.shape[1]).astype(F32)


def expert_sums(owned, adapters, owners, width, hidden):
    if owners <= RANK:
        return finish_expert_call(owned, adapters, owners, width, hidden)
    sums = [spread_expert_grads(value, adapters, owners) for value in owned]
    base = 3 * hidden
    up = [[value[:, 0:hidden], value[:, hidden : 2 * hidden]] for value in sums]
    down = [
        [value[:, base + width * part : base + width * (part + 1)].T for part in (1, 2)]
        for value in sums
    ]
    return (
        jnp.stack([jnp.stack(value) for value in down]),
        jnp.stack([jnp.stack(value) for value in up]),
        jnp.stack([value[:, 2 * hidden : base].T for value in sums]),
        jnp.stack([value[:, base : base + width] for value in sums]),
    )


def finish_adapter_body(adapters, in_ref, down_ref, up_ref):
    half = in_ref.shape[3]
    count = RANK * adapters

    def place(value):
        return value % adapters * RANK + value // adapters

    move = hot(iota((count, count), 0) == place(iota((count, count), 1)))
    back = hot(iota((count, count), 1) == place(iota((count, count), 0)))
    for part in range(2):
        span = slice(part * half, part * half + half)
        for kind in range(2):
            for index in range(4):
                first = (kind * 4 + index) * adapters
                rows = in_ref[:, part, first : first + adapters, :].astype(F32)
                rows = rows.reshape(count, half).astype(BF)
                if kind == 0:
                    down_ref[index, span, :] = mm_tn(rows, back)
                else:
                    up_ref[index, :, span] = mm(move, rows)


def sum_adapter_body(kinds, adapters, id_ref, in_ref, out_ref):
    count = in_ref.shape[0]
    column = iota((1, count), 1)
    found = jnp.zeros((1, count), jnp.int32)
    for source in range(count // kinds):
        found = jnp.where(column // kinds == source, id_ref[source], found)
    place = iota((adapters * kinds, count), 0)
    column = iota((adapters * kinds, count), 1)
    pick = hot((place % adapters == found) & (place // adapters == column % kinds))
    own = mm(pick, in_ref[...]).astype(BF)
    for index in range(out_ref.shape[0]):
        out_ref[index] = own


def adapter_sums(grads, meanwhile, ids, adapters, everyone, width):
    axes = ("dp", "expert")
    if everyone == 2 * RANK:
        kinds = 8
        got = exchange(grads.reshape(everyone, kinds, width // 2), axes)
        got, meanwhile = lax.optimization_barrier((got, meanwhile))
        own = pl.pallas_call(
            functools.partial(sum_adapter_body, kinds, adapters),
            in_specs=[smem(), pl.BlockSpec(memory_space=pltpu.VMEM)],
            out_shape=shape_of(everyone, kinds * adapters, width // 2),
            cost_estimate=cost(1e9, 5e6),
            name="adapter_gradient_part",
        )(ids, got.reshape(everyone * kinds, width // 2))
        full = exchange(own, axes).reshape(RANK, 2, 8 * adapters, width // 2)
        total = adapters * RANK
        down, upper = pl.pallas_call(
            functools.partial(finish_adapter_body, adapters),
            out_shape=[shape_of(4, width, total, dtype=F32), shape_of(4, total, width, dtype=F32)],
            cost_estimate=cost(1e9, 5e6),
            name="adapter_gradient_sums",
        )(full)
        return down, upper, meanwhile
    pieces = grads.reshape(everyone, RANK * 4 * 2 * width // everyone)
    got = exchange(pieces, axes)
    pick = (jnp.arange(adapters, dtype=jnp.int32)[:, None] == ids[None, :]).astype(BF)
    own = jnp.dot(pick, got, preferred_element_type=F32).astype(BF)
    full = gather_all(own, axes, everyone)
    full = full.reshape(RANK, everyone // RANK, adapters, -1).transpose(2, 0, 1, 3)
    full = full.reshape(adapters * RANK, 4, 2, width).astype(F32)
    return full[:, :, 0].transpose(1, 2, 0), full[:, :, 1].transpose(1, 0, 2), meanwhile


def body(
    tokens,
    cotangent,
    lengths,
    adapter_ids,
    routes,
    prev_logits,
    norm_gains,
    input_weights,
    output_weight,
    adapter_down,
    adapter_up,
    router,
    residual_mix,
    constant_mix,
    constant_vectors,
    expert_gate,
    expert_up,
    expert_down,
    expert_adapter_down,
    expert_adapter_up,
    output_adapter_down,
    output_adapter_up,
):
    tok_count, width = tokens.shape
    hidden_width = expert_gate.shape[2]
    group, owners = lax.axis_size("expert"), lax.axis_size("dp")
    local = expert_gate.shape[0]
    adapters = adapter_down.shape[-1] // RANK
    cosine, sine = (jnp.asarray(table) for table in turn_tables(tok_count))
    weights = (
        expert_gate, expert_up, expert_down, expert_adapter_down, expert_adapter_up,
        output_adapter_down, output_adapter_up,
    )
    per_owner = RANK // min(RANK, owners)
    everyone = owners * group
    me = lax.axis_index("expert")

    all_ids = exchange(jnp.broadcast_to(adapter_ids, (everyone,)), ("dp", "expert"))
    me = me.reshape(1).astype(jnp.int32)

    rows = jnp.concatenate(
        [prev_logits, routes.astype(F32), jnp.zeros((tok_count, 2), F32)], axis=1
    ).T
    slots, *grad_sends = route_call(local, group, lengths, me, rows, cotangent)
    cots = [swap(value, partner, group) for partner, value in enumerate(grad_sends)]
    small = jnp.concatenate(
        [
            router.astype(F32), jnp.zeros((width, MIX_ROW - EXPERTS - 4), F32), constant_mix,
            jnp.zeros((width, LANES - MIX_ROW - 4), F32),
        ],
        axis=1,
    )
    normed, inner, queries, keys, values, acat, bcat, table = pre_call(
        adapter_ids, tokens, norm_gains, input_weights, adapter_down, adapter_up, cosine, sine, small,
        constant_vectors,
    )
    queries, all_ids = lax.optimization_barrier((queries, all_ids))
    mixed, q2 = attend_call(lengths, queries, keys, values)
    mixed, cots = lax.optimization_barrier((mixed, cots))
    mixer = jnp.pad(residual_mix.T, ((0, 4), (0, 4)))
    hidden, ei, inner_o, data, cols = post_call(
        local, group, me, mixed, tokens, output_weight, acat, bcat, norm_gains, table, mixer, rows,
        slots,
    )
    sends = send_call(local, group, me, adapter_ids, slots, data, ei)
    near, far = tuple(range(group // 2)), tuple(range(group // 2, group))
    sent_near = [swap(sends[partner], partner, group) for partner in near]
    sent_far = [
        [swap(sends[group // 2 + place * local + index], partner, group) for place, partner in enumerate(far)]
        for index in range(local)
    ]
    backs = [[None] * group for _ in range(local)]
    results = [[None] * group for _ in range(local)]
    grads, last = [], None
    for index in range(local):
        before = None
        for pair in (near, far) if index % 2 == 0 else (far, near):
            pieces = sent_near if pair == near else sent_far[index]
            if last is not None:
                pieces, last = lax.optimization_barrier((pieces, last))
            if index == local - 1 and pair == near:
                pieces, backs[:index] = lax.optimization_barrier((pieces, backs[:index]))
            outs = expert_call(
                index, pair, group, per_owner, pieces, [cots[partner] for partner in pair], before, weights
            )
            before = last = outs[-1]
            for place, partner in enumerate(pair):
                backs[index][partner] = swap(outs[place], partner, group)
                results[index][partner] = outs[len(pair) + place]
        grads.append(before)
    backs = [value for some in backs for value in some]

    parts = [exchange_expert_grads(grad, group, owners) for grad in grads]
    sums = functools.partial(sum_expert_grads, me=me, ids=all_ids, adapters=adapters, group=group, owners=owners)
    parts[:-1], last = lax.optimization_barrier((parts[:-1], last))
    owned = [sums(part) for part in parts[:-1]]
    backs, owned = lax.optimization_barrier((backs, owned))
    back_hidden, back_attention, back_inner_o, back_mixed = combine_call(
        lengths, backs, rows, data, cols, cotangent, ei, hidden, norm_gains, output_weight, acat, bcat,
        table,
    )
    flat = [value for some in results for value in some]
    flat, back_mixed = lax.optimization_barrier((flat, back_mixed))
    flat = [swap(value, place % group, group) for place, value in enumerate(flat)]

    dq, dk, dv = attend_back_call(lengths, q2, keys, values, mixed, back_mixed, cosine, sine)
    parts[-1], dq = lax.optimization_barrier((parts[-1], dq))
    owned.append(sums(parts[-1]))
    dq, owned = lax.optimization_barrier((dq, owned))
    input_back, adapter_grads = last_call(
        everyone == 2 * RANK, dq, dk, dv, input_weights, acat, bcat, normed, inner, mixed, inner_o,
        back_attention, back_inner_o, tokens, back_hidden, norm_gains,
    )
    layer_out = result_call(lengths, flat, cols, ei, hidden, table)
    down_sum, upper_sum, layer_out = adapter_sums(
        adapter_grads, layer_out, all_ids, adapters, everyone, width
    )
    in_down_sum, in_up_sum, out_down_sum, out_up_sum = expert_sums(
        owned, adapters, owners, width, hidden_width
    )
    return (
        layer_out,
        input_back,
        down_sum,
        upper_sum,
        in_down_sum,
        in_up_sum,
        out_down_sum,
        out_up_sum,
    )


def solution(mesh):
    tokens_spec, copied = P(("dp", "expert"), None), P()
    owned = P("expert")
    placed = (
        (tokens_spec, tokens_spec, P(("dp", "expert")), P(("dp", "expert")), tokens_spec, tokens_spec)
        + (copied,) * 9
        + (owned,) * 7
    )
    return jax.shard_map(
        body,
        mesh=mesh,
        in_specs=placed,
        out_specs=(tokens_spec, tokens_spec, copied, copied) + (owned,) * 4,
        check_vma=False,
    )
```

time: 937 us -> 419 us (0.45)
  matrix products: 330 us -> 0 us
  Pallas kernels: 0 us -> 225 us
  other arithmetic: 216 us -> 4.38 us
  local copies, waits for them, and re-layouts: 217 us -> 7.51 us
  waiting for transfers between devices: 129 us -> 57.2 us
  blocking collectives: 0 us -> 62.6 us
  starting transfers between devices: 21.7 us -> 38 us
    dot_general x67 -> x0, matrix products: 330 us -> none  [the longest x1 35.3 us: attend_back(): jnp.einsum('qhd,khd->hqk', back_mixed, values, preferred_element_type=jnp...]
    pallas_call x0 -> x19, Pallas kernels: none -> 225 us  [the longest x4 72.9 us: expert_call(): pl.pallas_call(functools.partial(expert_body, pair, per_owner, group, ste...]
    psum x2 -> x0, waiting for transfers between devices: 120 us -> none  [the longest x1 120 us: body(): lax.psum((jnp.stack([down_query, down_key, down_value, down_output]), jnp...]
    reduce_sum x12 -> x0, other arithmetic: 115 us -> none  [the longest x1 40.3 us: body(): back_gates = jnp.sum(back_out[:, None, :] * outputs_all, axis=-1)]
    all_to_all x0 -> x1, blocking collectives: none -> 62.6 us  [exchange(): return lax.all_to_all(value, axes, split_axis=0, concat_axis=0, tiled=True)]
    gather x6 -> x0, local copies, waits for them, and re-layouts: 58.2 us -> none  [the longest x1 13 us: body(): padded_rows[target].reshape(tok_count, 2, model_width)]
    convert_element_type x12 -> x1, other arithmetic: 56.7 us -> 0.7 us  [body(): routes.astype(F32)]
    ppermute x0 -> x20, waiting for transfers between devices: none -> 50.4 us  [swap(): lax.ppermute(value, 'expert', [(index, index ^ partner) for index in rang...]
  transfers between devices with their start and end apart: 7 -> 26, of which waited for: 3 -> 10; matrix products, arithmetic and copies ran while one was open for 67% -> 1% of each run, Pallas kernels for 0% -> 43%
where the time goes in v1:
time: 419 us; the launch traced here: 411 us
  Pallas kernels  225 us (54%)
  blocking collectives  62.6 us (15%)
  waiting for transfers between devices  57.2 us (14%)
  starting transfers between devices  38 us (9%)
  between operations  16.2 us (4%)
  local copies, waits for them, and re-layouts  7.51 us (2%)
  other arithmetic  4.38 us (1%)
    pallas_call x4, Pallas kernels, expert_call(): pl.pallas_call(functools.partial(expert_body, pair, per_owner, group, ste...  72.9 us
    all_to_all x1, blocking collectives, exchange(): return lax.all_to_all(value, axes, split_axis=0, concat_axis=0, tiled=True)  62.6 us
    ppermute x20, waiting for transfers between devices, swap(): lax.ppermute(value, 'expert', [(index, index ^ partner) for index in rang...  50.4 us
    pallas_call x1, Pallas kernels, attend_back_call(): pl.pallas_call(attend_back_body, grid=(PAIRS,), in_specs=[smem(), pl.Bloc...  26.3 us
    pallas_call x1, Pallas kernels, combine_call(): pl.pallas_call(functools.partial(combine_body, pieces), grid=(tok_count /...  24 us
    pallas_call x1, Pallas kernels, attend_call(): pl.pallas_call(attend_body, grid=(PAIRS,), in_specs=[smem(), column, colu...  22.9 us
    all_to_all x4, starting transfers between devices, exchange(): return lax.all_to_all(value, axes, split_axis=0, concat_axis=0, tiled=True)  22.6 us
    ppermute x20, starting transfers between devices, swap(): lax.ppermute(value, 'expert', [(index, index ^ partner) for index in rang...  15.2 us
  transfers between devices with their start and end apart: 26, of which 10 were waited for; matrix products, arithmetic and copies ran while one was open for 1% of the time, Pallas kernels for 43%

profile of v1, /device:TPU:0, one launch (start us, length us, event | category | flops | bytes accessed | tf_op | source)
XLA Modules:
  0.0 410.5 jit_solution(16797058451613292327)
XLA Ops:
  7.9 0.7 convert_element_type.8
  8.6 1.5 maximum_bitcast_fusion.rows_ref.refs_8_
  10.2 6.5 %route_rows.1 = (s32[8,1024]{1,0:T(8,128)}, bf16[384,768]{1,0:T(8,128)(2,1)}, bf16[384,768]{1,0:T(8,128)(2,1)}, bf16[384,768]{1,0:T(8,128)(2,1)}, bf16[384,768]{1,0:T(8,128)(2,1)}) custom-call(s32[1]{0:T(128)S(6)} %copy.49.len_ref, s32[1]{0:T(128)} %bitcast.me_ref, f32[16,1024]{1,0:T(8,128)} %maximum_bitcast_fusion.rows_ref.refs_8_, bf16[1024,768]{1,0:T(8,128)(2,1)} %refs_11_.1), custom_call_target="tpu_custom_call" | custom-call | flops 1 | bytes 1 | tf_op jit(solution)/shard_map/route_rows/pallas_call | solution.py:151
  17.1 2.5 collective-permute-start.1
  21.0 6.1 %all-to-all-start = ((s32[32,1,1]{2,1,0:T(1,128)}), s32[32,1,1]{2,1,0:T(1,128)S(1)}, u32[]{:S(2)}, u32[]{:S(2)}) async-start(s32[32,1,1]{2,1,0:T(1,128)} %broadcast_in_dim.20), calls=%async_computation | async-start | bytes 32768 | tf_op jit(solution)/shard_map/all_to_all | solution.py:888
  27.6 0.9 maximum_maximum_fusion.small_ref
  28.6 12.5 %before_attention.1 = (bf16[1024,768]{1,0:T(8,128)(2,1)}, bf16[1024,128]{1,0:T(8,128)(2,1)}, bf16[1024,768]{1,0:T(8,128)(2,1)}, bf16[1024,768]{1,0:T(8,128)(2,1)...) custom-call(s32[1]{0:T(128)} %copy.50.id_ref, ...), custom_call_target="tpu_custom_call" | custom-call | flops 1 | bytes 1 | tf_op jit(solution)/shard_map/before_attention/pallas_call | solution.py:246
  41.8 6.1 %all-to-all-done = s32[32,1,1]{2,1,0:T(1,128)S(1)} async-done(((s32[32,1,1]{2,1,0:T(1,128)}), s32[32,1,1]{2,1,0:T(1,128)S(1)}, u32[]{:S(2)}, u32[]{:S(2)}) %all-to-all-start) | async-done | bytes 160 | tf_op jit(solution)/shard_map/all_to_all | solution.py:888
  47.8 1.2 reduce.id_ref
  49.1 22.9 %attention_forward.1 = (bf16[1024,768]{1,0:T(8,128)(2,1)}, bf16[1024,1536]{1,0:T(8,128)(2,1)}) custom-call(s32[1]{0:T(128)S(6)} %copy.49.len_ref, bf16[1024,768]{1,0:T(8,128)(2,1)} %get-tuple-element.120.q_ref, bf16[1024,768]{1,0:T(8,128)(2,1)} %get-tuple-element.121.k_ref, bf16[1024,768]{1,0:T(8,128)(2,1)} %get-tuple-element.122.v_ref), custom_call_target="tpu_custom_call" | custom-call | flops 1 | bytes 1 | tf_op jit(solution)/shard_map/attention_forward/pallas_call | solution.py:310
  72.1 10.5 %after_attention.1 = (f32[1024,768]{1,0:T(8,128)}, bf16[1024,768]{1,0:T(8,128)(2,1)}, bf16[1024,128]{1,0:T(8,128)(2,1)}, f32[16,1024]{1,0:T(8,128)}, f32[1024,128]{1,0:T(8,128)}) custom-call(s32[1]{0:T(128)} %bitcast.me_ref, bf16[1024,768]{1,0:T(8,128)(2,1)} %get-tuple-element.128.mixed_ref, bf16[1024,768]{1,0:T(8,128)(2,1)} %x_ref.5, ...), custom_call_target="tpu_custom_call" | custom-call | flops 1 | bytes 1 | tf_op jit(solution)/shard_map/after_attention/pallas_call | solution.py:466
  82.6 8.4 %send_rows.1 = (bf16[400,768]{1,0:T(8,128)(2,1)}, bf16[400,768]{1,0:T(8,128)(2,1)}, bf16[200,768]{1,0:T(8,128)(2,1)}, bf16[200,768]{1,0:T(8,128)(2,1)}, bf16[200...) custom-call(s32[1]{0:T(128)} %bitcast.me_ref, s32[1]{0:T(128)} %copy.50.id_ref, s32[8,1024]{1,0:T(8,128)} %get-tuple-element.118.slot_ref, ...), custom_call_target="tpu_custom_call" | custom-call | flops 1 | bytes 1 | tf_op jit(solution)/shard_map/send_rows/pallas_call | solution.py:190
  91.0 1.5 collective-permute-start.6
  93.2 0.8 copy-done.2
  94.1 18.1 %expert_layer.4 = (bf16[200,768]{1,0:T(8,128)(2,1)}, bf16[200,768]{1,0:T(8,128)(2,1)}, bf16[192,768]{1,0:T(8,128)(2,1)}, bf16[192,768]{1,0:T(8,128)(2,1)}, bf16[64,8448]{1,0:T(8,128)(2,1)}) custom-call(bf16[400,768]{1,0:T(8,128)(2,1)} %get-tuple-element.157.refs_0_, bf16[400,768]{1,0:T(8,128)(2,1)} %copy-done.2, ...), custom_call_target="tpu_custom_call" | custom-call | flops 1 | bytes 1 | tf_op jit(solution)/shard_map/expert_layer/pallas_call | solution.py:610
  113.0 18.3 %expert_layer.5 = (bf16[200,768]{1,0:T(8,128)(2,1)}, bf16[200,768]{1,0:T(8,128)(2,1)}, bf16[192,768]{1,0:T(8,128)(2,1)}, bf16[192,768]{1,0:T(8,128)(2,1)}, bf16[64,8448]{1,0:T(8,128)(2,1)}) custom-call(bf16[200,768]{1,0:T(8,128)(2,1)} %copy-done.15, bf16[200,768]{1,0:T(8,128)(2,1)} %copy-done.16, bf16[384,768]{1,0:T(8,128)(2,1)} %copy-done.4, ...), custom_call_target="tpu_custom_call" | custom-call | flops 1 | bytes 1 | tf_op jit(solution)/shard_map/expert_layer/pallas_call | solution.py:610
  131.3 5.3 %all-to-all-start.2 = ((bf16[8,8,8448]{2,1,0:T(8,128)(2,1)}), bf16[8,8,8448]{2,1,0:T(8,128)(2,1)S(1)}, u32[]{:S(2)}, u32[]{:S(2)}) async-start(bf16[8,8,8448]{2,1,0:T(8,128)(2,1)} %bitcast.21), calls=%async_computation.2 | async-start | bytes 2162688 | tf_op jit(solution)/shard_map/all_to_all | solution.py:888
  136.6 1.5 collective-permute-start.4
  138.8 1.5 collective-permute-start.9
  140.3 6.5 %collective-permute-done.4.refs_0_ = bf16[200,768]{1,0:T(8,128)(2,1)S(1)} collective-permute-done((bf16[200,768]{1,0:T(8,128)(2,1)S(1)}, bf16[200,768]{1,0:T(8,128)(2,1)S(1)}, u32[]{:S(2)}, u32[]{:S(2)}) %collective-permute-start.4) | collective-permute-done | bytes 307232 | tf_op jit(solution)/shard_map/ppermute | solution.py:898
  146.8 5.6 %collective-permute-done.5.refs_1_ = bf16[200,768]{1,0:T(8,128)(2,1)S(1)} collective-permute-done((bf16[200,768]{1,0:T(8,128)(2,1)S(1)}, bf16[200,768]{1,0:T(8,128)(2,1)S(1)}, u32[]{:S(2)}, u32[]{:S(2)}) %collective-permute-start.5) | collective-permute-done | bytes 307232 | tf_op jit(solution)/shard_map/ppermute | solution.py:898
  152.4 0.7 copy-done.8
  153.1 17.9 %expert_layer.6 = (bf16[200,768]{1,0:T(8,128)(2,1)}, bf16[200,768]{1,0:T(8,128)(2,1)}, bf16[192,768]{1,0:T(8,128)(2,1)}, bf16[192,768]{1,0:T(8,128)(2,1)}, bf16[64,8448]{1,0:T(8,128)(2,1)}) custom-call(bf16[200,768]{1,0:T(8,128)(2,1)} %copy-done.7, bf16[200,768]{1,0:T(8,128)(2,1)} %copy-done.8, bf16[384,768]{1,0:T(8,128)(2,1)} %copy-done.4, ...), custom_call_target="tpu_custom_call" | custom-call | flops 1 | bytes 1 | tf_op jit(solution)/shard_map/expert_layer/pallas_call | solution.py:610
  171.1 18.6 %expert_layer.7 = (bf16[200,768]{1,0:T(8,128)(2,1)}, bf16[200,768]{1,0:T(8,128)(2,1)}, bf16[192,768]{1,0:T(8,128)(2,1)}, bf16[192,768]{1,0:T(8,128)(2,1)}, bf16[64,8448]{1,0:T(8,128)(2,1)}) custom-call(bf16[400,768]{1,0:T(8,128)(2,1)} %get-tuple-element.157.refs_0_, bf16[400,768]{1,0:T(8,128)(2,1)} %copy-done.2, ...), custom_call_target="tpu_custom_call" | custom-call | flops 1 | bytes 1 | tf_op jit(solution)/shard_map/expert_layer/pallas_call | solution.py:610
  189.7 6.2 %all-to-all-start.1 = ((bf16[8,8,8448]{2,1,0:T(8,128)(2,1)}), bf16[8,8,8448]{2,1,0:T(8,128)(2,1)S(1)}, u32[]{:S(2)}, u32[]{:S(2)}) async-start(bf16[8,8,8448]{2,1,0:T(8,128)(2,1)} %bitcast.20), calls=%async_computation.1 | async-start | bytes 2162688 | tf_op jit(solution)/shard_map/all_to_all | solution.py:888
  196.6 1.6 collective-permute-start.13
  198.2 2.2 expert_gradient_part.2
  200.5 5.9 %collective-permute-done.12.refs_6_ = bf16[200,768]{1,0:T(8,128)(2,1)S(1)} collective-permute-done((bf16[200,768]{1,0:T(8,128)(2,1)}, bf16[200,768]{1,0:T(8,128)(2,1)S(1)}, u32[]{:S(2)}, u32[]{:S(2)}) %collective-permute-start.12) | collective-permute-done | bytes 307232 | tf_op jit(solution)/shard_map/ppermute | solution.py:898
  206.4 6.3 %collective-permute-done.13.refs_7_ = bf16[200,768]{1,0:T(8,128)(2,1)S(1)} collective-permute-done((bf16[200,768]{1,0:T(8,128)(2,1)S(1)}, bf16[200,768]{1,0:T(8,128)(2,1)S(1)}, u32[]{:S(2)}, u32[]{:S(2)}) %collective-permute-start.13) | collective-permute-done | bytes 307232 | tf_op jit(solution)/shard_map/ppermute | solution.py:898
  213.6 24.0 %combine_backward.1 = (f32[1024,768]{1,0:T(8,128)}, bf16[1024,768]{1,0:T(8,128)(2,1)}, bf16[1024,128]{1,0:T(8,128)(2,1)}, bf16[1024,768]{1,0:T(8,128)(2,1)}) custom-call(s32[1]{0:T(128)S(6)} %copy.49.len_ref, bf16[200,768]{1,0:T(8,128)(2,1)} %get-tuple-element.179.refs_0_, bf16[200,768]{1,0:T(8,128)(2,1)} %copy-done.9, bf16[200,768]{1,0:T(8,128)(2,1)} %copy-done.10, ...), custom_call_target="tpu_custom_call" | custom-call | flops 1 | bytes 1 | tf_op jit(solution)/shard_map/combine_backward/pallas_call | solution.py:745
  237.6 26.3 %attention_backward.1 = (bf16[1024,768]{1,0:T(8,128)(2,1)}, bf16[1024,768]{1,0:T(8,128)(2,1)}, bf16[1024,768]{1,0:T(8,128)(2,1)}) custom-call(s32[1]{0:T(128)S(6)} %copy.49.len_ref, bf16[1024,1536]{1,0:T(8,128)(2,1)} %get-tuple-element.160.q2_ref, bf16[1024,768]{1,0:T(8,128)(2,1)} %get-tuple-element.121.k_ref, bf16[1024,768]{1,0:T(8,128)(2,1)} %get-tuple-element.122.v_ref, ...), custom_call_target="tpu_custom_call" | custom-call | flops 1 | bytes 1 | tf_op jit(solution)/shard_map/attention_backward/pallas_call | solution.py:385
  263.8 1.0 copy-done.1
  264.8 2.2 expert_gradient_part.3
  268.1 13.9 %after_attention_backward.1 = (bf16[1024,768]{1,0:T(8,128)(2,1)}, bf16[256,384]{1,0:T(8,128)(2,1)}) custom-call(bf16[1024,768]{1,0:T(8,128)(2,1)} %get-tuple-element.195.dq_ref, bf16[1024,768]{1,0:T(8,128)(2,1)} %get-tuple-element.196.dk_ref, bf16[1024,768]{1,0:T(8,128)(2,1)} %get-tuple-element.197.dv_ref, bf16[3,768,768]{2,1,0:T(8,128)(2,1)} %w_ref.3, ...), custom_call_target="tpu_custom_call" | custom-call | flops 1 | bytes 1 | tf_op jit(solution)/shard_map/after_attention_backward/pallas_call | solution.py:869
  282.0 5.1 %all-to-all-start.3 = ((bf16[32,8,384]{2,1,0:T(8,128)(2,1)}), bf16[32,8,384]{2,1,0:T(8,128)(2,1)S(1)}, u32[]{:S(2)}, u32[]{:S(2)}) async-start(bf16[32,8,384]{2,1,0:T(8,128)(2,1)} %bitcast.23), calls=%async_computation.3 | async-start | bytes 393216 | tf_op jit(solution)/shard_map/all_to_all | solution.py:888
  287.2 1.8 collective-permute-start.15
  289.4 1.8 collective-permute-start.18
  291.2 7.7 %collective-permute-done.15.refs_2_ = bf16[192,768]{1,0:T(8,128)(2,1)S(1)} collective-permute-done((bf16[192,768]{1,0:T(8,128)(2,1)S(1)}, bf16[192,768]{1,0:T(8,128)(2,1)S(1)}, u32[]{:S(2)}, u32[]{:S(2)}) %collective-permute-start.15) | collective-permute-done | bytes 294944 | tf_op jit(solution)/shard_map/ppermute | solution.py:898
  298.9 5.4 %collective-permute-done.16.refs_3_ = bf16[192,768]{1,0:T(8,128)(2,1)S(1)} collective-permute-done((bf16[192,768]{1,0:T(8,128)(2,1)S(1)}, bf16[192,768]{1,0:T(8,128)(2,1)S(1)}, u32[]{:S(2)}, u32[]{:S(2)}) %collective-permute-start.16) | collective-permute-done | bytes 294944 | tf_op jit(solution)/shard_map/ppermute | solution.py:898
  304.3 7.3 %collective-permute-done.18.refs_6_ = bf16[192,768]{1,0:T(8,128)(2,1)S(1)} collective-permute-done((bf16[192,768]{1,0:T(8,128)(2,1)}, bf16[192,768]{1,0:T(8,128)(2,1)S(1)}, u32[]{:S(2)}, u32[]{:S(2)}) %collective-permute-start.18) | collective-permute-done | bytes 294944 | tf_op jit(solution)/shard_map/ppermute | solution.py:898
  311.6 5.4 %collective-permute-done.19.refs_7_ = bf16[192,768]{1,0:T(8,128)(2,1)S(1)} collective-permute-done((bf16[192,768]{1,0:T(8,128)(2,1)S(1)}, bf16[192,768]{1,0:T(8,128)(2,1)S(1)}, u32[]{:S(2)}, u32[]{:S(2)}) %collective-permute-start.19) | collective-permute-done | bytes 294944 | tf_op jit(solution)/shard_map/ppermute | solution.py:898
  317.0 0.7 copy-done.22
  317.7 8.0 %layer_output.1 = bf16[1024,768]{1,0:T(8,128)(2,1)} custom-call(s32[1]{0:T(128)S(6)} %copy.49.len_ref, bf16[192,768]{1,0:T(8,128)(2,1)} %get-tuple-element.205.refs_0_, bf16[192,768]{1,0:T(8,128)(2,1)} %copy-done.17, bf16[192,768]{1,0:T(8,128)(2,1)} %copy-done.18, bf16[192,768]{1,0:T(8,128)(2,1)} %copy-done.19, bf16[192,768]{1,0:T(8,128)(2,1)} %get-tuple-element.209.refs_4_, ...), custom_call_target="tpu_custom_call" | custom-call | flops 1 | bytes 1 | tf_op jit(solution)/shard_map/layer_output/pallas_call | solution.py:794
  326.3 2.5 adapter_gradient_part.1
  328.8 62.6 %all_to_all.29 = bf16[32,64,384]{2,1,0:T(8,128)(2,1)} all-to-all(bf16[32,64,384]{2,1,0:T(8,128)(2,1)} %adapter_gradient_part.1), channel_id=1, replica_groups=mesh['dp'=8,'expert'=4] {'dp','expert'}, dimensions={0} | all-to-all | bytes 3145728 | tf_op jit(solution)/shard_map/all_to_all | solution.py:888
  391.5 3.6 adapter_gradient_sums.1
  395.0 4.1 expert_gradient_sums.2
  399.1 4.1 expert_gradient_sums.3
  (109 shorter events, 8.5 us)
Async XLA Ops:
  7.2 20.1 %copy-start.23 = (bf16[768,12]{0,1:T(8,128)(2,1)S(1)}, bf16[768,12]{0,1:T(8,128)(2,1)}, u32[]{:S(2)}) copy-start(bf16[768,12]{0,1:T(8,128)(2,1)} %param.35) | copy-start | bytes 55300
  7.2 20.3 %copy-start.24 = (f32[768,4]{0,1:T(4,128)S(1)}, f32[768,4]{0,1:T(4,128)}, u32[]{:S(2)}) copy-start(f32[768,4]{0,1:T(4,128)} %param.37) | copy-start | bytes 36868
  16.7 55.3 %collective-permute-start = (bf16[384,768]{1,0:T(8,128)(2,1)}, bf16[384,768]{1,0:T(8,128)(2,1)S(1)}, u32[]{:S(2)}, u32[]{:S(2)}) collective-permute-start(bf16[384,768]{1,0:T(8,128)(2,1)} %get-tuple-element.125), channel_id=1, source_target_pairs={{0,1},{1,0},{2,3},{3,2},{4,5},{5,4},{6,7},{7,6},{8,9},{9,8},{10,11... | collective-permute-start | bytes 1769480 | tf_op jit(solution)/shard_map/ppermute | solution.py:898
  17.1 54.9 %collective-permute-start.1 = (bf16[384,768]{1,0:T(8,128)(2,1)}, bf16[384,768]{1,0:T(8,128)(2,1)S(1)}, u32[]{:S(2)}, u32[]{:S(2)}) collective-permute-start(bf16[384,768]{1,0:T(8,128)(2,1)} %get-tuple-element.126), channel_id=1, source_target_pairs={{0,2},{1,3},{2,0},{3,1},{4,6},{5,7},{6,4},{7,5},{8,10},{9,11},{10,... | collective-permute-start | bytes 1769480 | tf_op jit(solution)/shard_map/ppermute | solution.py:898
  19.6 52.4 %collective-permute-start.2 = (bf16[384,768]{1,0:T(8,128)(2,1)}, bf16[384,768]{1,0:T(8,128)(2,1)S(1)}, u32[]{:S(2)}, u32[]{:S(2)}) collective-permute-start(bf16[384,768]{1,0:T(8,128)(2,1)} %get-tuple-element.127), channel_id=1, source_target_pairs={{0,3},{1,2},{2,1},{3,0},{4,7},{5,6},{6,5},{7,4},{8,11},{9,10},{10,... | collective-permute-start | bytes 1769480 | tf_op jit(solution)/shard_map/ppermute | solution.py:898
  21.0 26.8 %all-to-all-start = ((s32[32,1,1]{2,1,0:T(1,128)}), s32[32,1,1]{2,1,0:T(1,128)S(1)}, u32[]{:S(2)}, u32[]{:S(2)}) async-start(s32[32,1,1]{2,1,0:T(1,128)} %broadcast_in_dim.20), calls=%async_computation | async-start | bytes 32768 | tf_op jit(solution)/shard_map/all_to_all | solution.py:888
  28.6 12.5 %copy-start.25 = (f32[12,12]{1,0:T(8,128)S(1)}, f32[12,12]{1,0:T(8,128)}, u32[]{:S(2)}) copy-start(f32[12,12]{1,0:T(8,128)} %param.36) | copy-start | bytes 1732
  72.0 10.6 %copy-start.3 = (bf16[384,768]{1,0:T(8,128)(2,1)}, bf16[384,768]{1,0:T(8,128)(2,1)S(1)}, u32[]{:S(2)}) copy-start(bf16[384,768]{1,0:T(8,128)(2,1)S(1)} %collective-permute-done.refs_3_) | copy-start | bytes 1769476
  72.0 10.5 %copy-start.4 = (bf16[384,768]{1,0:T(8,128)(2,1)}, bf16[384,768]{1,0:T(8,128)(2,1)S(1)}, u32[]{:S(2)}) copy-start(bf16[384,768]{1,0:T(8,128)(2,1)S(1)} %collective-permute-done.1.refs_2_) | copy-start | bytes 1769476
  72.0 10.5 %copy-start.5 = (bf16[384,768]{1,0:T(8,128)(2,1)}, bf16[384,768]{1,0:T(8,128)(2,1)S(1)}, u32[]{:S(2)}) copy-start(bf16[384,768]{1,0:T(8,128)(2,1)S(1)} %collective-permute-done.2.refs_3_) | copy-start | bytes 1769476
  91.0 2.2 collective-permute-start.3
  91.0 21.2 %collective-permute-start.6 = (bf16[200,768]{1,0:T(8,128)(2,1)}, bf16[200,768]{1,0:T(8,128)(2,1)S(1)}, u32[]{:S(2)}, u32[]{:S(2)}) collective-permute-start(bf16[200,768]{1,0:T(8,128)(2,1)} %get-tuple-element.138), channel_id=1, source_target_pairs={{0,2},{1,3},{2,0},{3,1},{4,6},{5,7},{6,4},{7,5},{8,10},{9,11},{10,... | collective-permute-start | bytes 921608 | tf_op jit(solution)/shard_map/ppermute | solution.py:898
  92.5 19.7 %collective-permute-start.7 = (bf16[200,768]{1,0:T(8,128)(2,1)}, bf16[200,768]{1,0:T(8,128)(2,1)S(1)}, u32[]{:S(2)}, u32[]{:S(2)}) collective-permute-start(bf16[200,768]{1,0:T(8,128)(2,1)} %get-tuple-element.139), channel_id=1, source_target_pairs={{0,3},{1,2},{2,1},{3,0},{4,7},{5,6},{6,5},{7,4},{8,11},{9,10},{10,... | collective-permute-start | bytes 921608 | tf_op jit(solution)/shard_map/ppermute | solution.py:898
  131.3 6.8 %copy-start.26 = (bf16[200,768]{1,0:T(8,128)(2,1)S(1)}, bf16[200,768]{1,0:T(8,128)(2,1)}, u32[]{:S(2)}) copy-start(bf16[200,768]{1,0:T(8,128)(2,1)} %get-tuple-element.137) | copy-start | bytes 921604
  131.3 6.8 %copy-start.28 = (bf16[200,768]{1,0:T(8,128)(2,1)S(1)}, bf16[200,768]{1,0:T(8,128)(2,1)}, u32[]{:S(2)}) copy-start(bf16[200,768]{1,0:T(8,128)(2,1)} %get-tuple-element.154) | copy-start | bytes 921604
  131.3 58.4 %all-to-all-start.2 = ((bf16[8,8,8448]{2,1,0:T(8,128)(2,1)}), bf16[8,8,8448]{2,1,0:T(8,128)(2,1)S(1)}, u32[]{:S(2)}, u32[]{:S(2)}) async-start(bf16[8,8,8448]{2,1,0:T(8,128)(2,1)} %bitcast.21), calls=%async_computation.2 | async-start | bytes 2162688 | tf_op jit(solution)/shard_map/all_to_all | solution.py:888
  136.6 10.2 %collective-permute-start.4 = (bf16[200,768]{1,0:T(8,128)(2,1)S(1)}, bf16[200,768]{1,0:T(8,128)(2,1)S(1)}, u32[]{:S(2)}, u32[]{:S(2)}) collective-permute-start(bf16[200,768]{1,0:T(8,128)(2,1)S(1)} %copy-done.27), channel_id=1, source_target_pairs={{0,2},{1,3},{2,0},{3,1},{4,6},{5,7},{6,4},{7,5},{8,10},{9,11},{10,... | collective-permute-start | bytes 921608 | tf_op jit(solution)/shard_map/ppermute | solution.py:898
  138.1 14.3 %collective-permute-start.5 = (bf16[200,768]{1,0:T(8,128)(2,1)S(1)}, bf16[200,768]{1,0:T(8,128)(2,1)S(1)}, u32[]{:S(2)}, u32[]{:S(2)}) collective-permute-start(bf16[200,768]{1,0:T(8,128)(2,1)S(1)} %copy-done.26), channel_id=1, source_target_pairs={{0,3},{1,2},{2,1},{3,0},{4,7},{5,6},{6,5},{7,4},{8,11},{9,10},{10,... | collective-permute-start | bytes 921608 | tf_op jit(solution)/shard_map/ppermute | solution.py:898
  138.2 32.9 %collective-permute-start.8 = (bf16[200,768]{1,0:T(8,128)(2,1)S(1)}, bf16[200,768]{1,0:T(8,128)(2,1)S(1)}, u32[]{:S(2)}, u32[]{:S(2)}) collective-permute-start(bf16[200,768]{1,0:T(8,128)(2,1)S(1)} %copy-done.28), channel_id=1, source_target_pairs={{0,1},{1,0},{2,3},{3,2},{4,5},{5,4},{6,7},{7,6},{8,9},{9,8},{10,11... | collective-permute-start | bytes 921608 | tf_op jit(solution)/shard_map/ppermute | solution.py:898
  138.8 32.2 %collective-permute-start.9 = (bf16[200,768]{1,0:T(8,128)(2,1)}, bf16[200,768]{1,0:T(8,128)(2,1)S(1)}, u32[]{:S(2)}, u32[]{:S(2)}) collective-permute-start(bf16[200,768]{1,0:T(8,128)(2,1)} %get-tuple-element.155), channel_id=1, source_target_pairs={{0,2},{1,3},{2,0},{3,1},{4,6},{5,7},{6,4},{7,5},{8,10},{9,11},{10,... | collective-permute-start | bytes 921608 | tf_op jit(solution)/shard_map/ppermute | solution.py:898
  140.3 30.8 %collective-permute-start.10 = (bf16[200,768]{1,0:T(8,128)(2,1)}, bf16[200,768]{1,0:T(8,128)(2,1)S(1)}, u32[]{:S(2)}, u32[]{:S(2)}) collective-permute-start(bf16[200,768]{1,0:T(8,128)(2,1)} %get-tuple-element.156), channel_id=1, source_target_pairs={{0,3},{1,2},{2,1},{3,0},{4,7},{5,6},{6,5},{7,4},{8,11},{9,10},{10,... | collective-permute-start | bytes 921608 | tf_op jit(solution)/shard_map/ppermute | solution.py:898
  146.8 5.6 %copy-start.7 = (bf16[200,768]{1,0:T(8,128)(2,1)}, bf16[200,768]{1,0:T(8,128)(2,1)S(1)}, u32[]{:S(2)}) copy-start(bf16[200,768]{1,0:T(8,128)(2,1)S(1)} %collective-permute-done.4.refs_0_) | copy-start | bytes 921604
  171.0 18.6 %copy-start.9 = (bf16[200,768]{1,0:T(8,128)(2,1)}, bf16[200,768]{1,0:T(8,128)(2,1)S(1)}, u32[]{:S(2)}) copy-start(bf16[200,768]{1,0:T(8,128)(2,1)S(1)} %collective-permute-done.8.refs_1_) | copy-start | bytes 921604
  171.1 18.6 %copy-start.10 = (bf16[200,768]{1,0:T(8,128)(2,1)}, bf16[200,768]{1,0:T(8,128)(2,1)S(1)}, u32[]{:S(2)}) copy-start(bf16[200,768]{1,0:T(8,128)(2,1)S(1)} %collective-permute-done.9.refs_2_) | copy-start | bytes 921604
  171.1 18.6 %copy-start.11 = (bf16[200,768]{1,0:T(8,128)(2,1)}, bf16[200,768]{1,0:T(8,128)(2,1)S(1)}, u32[]{:S(2)}) copy-start(bf16[200,768]{1,0:T(8,128)(2,1)S(1)} %collective-permute-done.10.refs_3_) | copy-start | bytes 921604
  189.7 6.9 %copy-start.29 = (bf16[200,768]{1,0:T(8,128)(2,1)S(1)}, bf16[200,768]{1,0:T(8,128)(2,1)}, u32[]{:S(2)}) copy-start(bf16[200,768]{1,0:T(8,128)(2,1)} %get-tuple-element.176) | copy-start | bytes 921604
  189.7 8.5 %copy-start = (bf16[8,8,8448]{2,1,0:T(8,128)(2,1)}, bf16[8,8,8448]{2,1,0:T(8,128)(2,1)S(1)}, u32[]{:S(2)}) copy-start(bf16[8,8,8448]{2,1,0:T(8,128)(2,1)S(1)} %all-to-all-done.2) | copy-start | bytes 3244036
  189.7 74.1 %all-to-all-start.1 = ((bf16[8,8,8448]{2,1,0:T(8,128)(2,1)}), bf16[8,8,8448]{2,1,0:T(8,128)(2,1)S(1)}, u32[]{:S(2)}, u32[]{:S(2)}) async-start(bf16[8,8,8448]{2,1,0:T(8,128)(2,1)} %bitcast.20), calls=%async_computation.1 | async-start | bytes 2162688 | tf_op jit(solution)/shard_map/all_to_all | solution.py:888
  195.9 199.1 %all-gather.7.cloned.1.call-start = ((), (), s32[]{:S(2)}) async-start(), calls=%async_computation.6 | async-start | bytes 2433024 | tf_op jit(solution)/shard_map/all_gather | solution.py:966
  195.9 10.4 %collective-permute-start.12 = (bf16[200,768]{1,0:T(8,128)(2,1)}, bf16[200,768]{1,0:T(8,128)(2,1)S(1)}, u32[]{:S(2)}, u32[]{:S(2)}) collective-permute-start(bf16[200,768]{1,0:T(8,128)(2,1)} %get-tuple-element.175), channel_id=1, source_target_pairs={{0,2},{1,3},{2,0},{3,1},{4,6},{5,7},{6,4},{7,5},{8,10},{9,11},{10,... | collective-permute-start | bytes 921608 | tf_op jit(solution)/shard_map/ppermute | solution.py:898
  196.6 16.1 %collective-permute-start.13 = (bf16[200,768]{1,0:T(8,128)(2,1)S(1)}, bf16[200,768]{1,0:T(8,128)(2,1)S(1)}, u32[]{:S(2)}, u32[]{:S(2)}) collective-permute-start(bf16[200,768]{1,0:T(8,128)(2,1)S(1)} %copy-done.29), channel_id=1, source_target_pairs={{0,3},{1,2},{2,1},{3,0},{4,7},{5,6},{6,5},{7,4},{8,11},{9,10},{10,... | collective-permute-start | bytes 921608 | tf_op jit(solution)/shard_map/ppermute | solution.py:898
  198.2 14.5 %collective-permute-start.11 = (bf16[200,768]{1,0:T(8,128)(2,1)}, bf16[200,768]{1,0:T(8,128)(2,1)S(1)}, u32[]{:S(2)}, u32[]{:S(2)}) collective-permute-start(bf16[200,768]{1,0:T(8,128)(2,1)} %get-tuple-element.174), channel_id=1, source_target_pairs={{0,1},{1,0},{2,3},{3,2},{4,5},{5,4},{6,7},{7,6},{8,9},{9,8},{10,11... | collective-permute-start | bytes 921608 | tf_op jit(solution)/shard_map/ppermute | solution.py:898
  206.4 6.4 %copy-start.12 = (bf16[200,768]{1,0:T(8,128)(2,1)}, bf16[200,768]{1,0:T(8,128)(2,1)S(1)}, u32[]{:S(2)}) copy-start(bf16[200,768]{1,0:T(8,128)(2,1)S(1)} %collective-permute-done.12.refs_6_) | copy-start | bytes 921604
  267.1 132.1 %all-gather.5.cloned.1.call-start = ((), (), s32[]{:S(2)}) async-start(), calls=%async_computation.5 | async-start | bytes 2433024 | tf_op jit(solution)/shard_map/all_gather | solution.py:966
  267.8 23.3 %collective-permute-start.14 = (bf16[192,768]{1,0:T(8,128)(2,1)S(1)}, bf16[192,768]{1,0:T(8,128)(2,1)S(1)}, u32[]{:S(2)}, u32[]{:S(2)}) collective-permute-start(bf16[192,768]{1,0:T(8,128)(2,1)S(1)} %copy-done.30), channel_id=1, source_target_pairs={{0,1},{1,0},{2,3},{3,2},{4,5},{5,4},{6,7},{7,6},{8,9},{9,8},{10,11... | collective-permute-start | bytes 884744 | tf_op jit(solution)/shard_map/ppermute | solution.py:898
  268.1 19.0 %copy-start.32 = (bf16[192,768]{1,0:T(8,128)(2,1)S(1)}, bf16[192,768]{1,0:T(8,128)(2,1)}, u32[]{:S(2)}) copy-start(bf16[192,768]{1,0:T(8,128)(2,1)} %get-tuple-element.207) | copy-start | bytes 884740
  268.1 20.9 %copy-start.31 = (bf16[192,768]{1,0:T(8,128)(2,1)S(1)}, bf16[192,768]{1,0:T(8,128)(2,1)}, u32[]{:S(2)}) copy-start(bf16[192,768]{1,0:T(8,128)(2,1)} %get-tuple-element.208) | copy-start | bytes 884740
  268.1 23.0 %copy-start.33 = (bf16[192,768]{1,0:T(8,128)(2,1)S(1)}, bf16[192,768]{1,0:T(8,128)(2,1)}, u32[]{:S(2)}) copy-start(bf16[192,768]{1,0:T(8,128)(2,1)} %get-tuple-element.212) | copy-start | bytes 884740
  282.0 43.6 %all-to-all-start.3 = ((bf16[32,8,384]{2,1,0:T(8,128)(2,1)}), bf16[32,8,384]{2,1,0:T(8,128)(2,1)S(1)}, u32[]{:S(2)}, u32[]{:S(2)}) async-start(bf16[32,8,384]{2,1,0:T(8,128)(2,1)} %bitcast.23), calls=%async_computation.3 | async-start | bytes 393216 | tf_op jit(solution)/shard_map/all_to_all | solution.py:888
  287.2 11.8 %collective-permute-start.15 = (bf16[192,768]{1,0:T(8,128)(2,1)S(1)}, bf16[192,768]{1,0:T(8,128)(2,1)S(1)}, u32[]{:S(2)}, u32[]{:S(2)}) collective-permute-start(bf16[192,768]{1,0:T(8,128)(2,1)S(1)} %copy-done.32), channel_id=1, source_target_pairs={{0,2},{1,3},{2,0},{3,1},{4,6},{5,7},{6,4},{7,5},{8,10},{9,11},{10,... | collective-permute-start | bytes 884744 | tf_op jit(solution)/shard_map/ppermute | solution.py:898
  289.0 15.3 %collective-permute-start.16 = (bf16[192,768]{1,0:T(8,128)(2,1)S(1)}, bf16[192,768]{1,0:T(8,128)(2,1)S(1)}, u32[]{:S(2)}, u32[]{:S(2)}) collective-permute-start(bf16[192,768]{1,0:T(8,128)(2,1)S(1)} %copy-done.31), channel_id=1, source_target_pairs={{0,3},{1,2},{2,1},{3,0},{4,7},{5,6},{6,5},{7,4},{8,11},{9,10},{10,... | collective-permute-start | bytes 884744 | tf_op jit(solution)/shard_map/ppermute | solution.py:898
  289.0 15.3 %collective-permute-start.17 = (bf16[192,768]{1,0:T(8,128)(2,1)}, bf16[192,768]{1,0:T(8,128)(2,1)S(1)}, u32[]{:S(2)}, u32[]{:S(2)}) collective-permute-start(bf16[192,768]{1,0:T(8,128)(2,1)} %get-tuple-element.210), channel_id=1, source_target_pairs={{0,1},{1,0},{2,3},{3,2},{4,5},{5,4},{6,7},{7,6},{8,9},{9,8},{10,11... | collective-permute-start | bytes 884744 | tf_op jit(solution)/shard_map/ppermute | solution.py:898
  289.4 22.2 %collective-permute-start.18 = (bf16[192,768]{1,0:T(8,128)(2,1)}, bf16[192,768]{1,0:T(8,128)(2,1)S(1)}, u32[]{:S(2)}, u32[]{:S(2)}) collective-permute-start(bf16[192,768]{1,0:T(8,128)(2,1)} %get-tuple-element.211), channel_id=1, source_target_pairs={{0,2},{1,3},{2,0},{3,1},{4,6},{5,7},{6,4},{7,5},{8,10},{9,11},{10,... | collective-permute-start | bytes 884744 | tf_op jit(solution)/shard_map/ppermute | solution.py:898
  291.2 25.8 %copy-start.17 = (bf16[192,768]{1,0:T(8,128)(2,1)}, bf16[192,768]{1,0:T(8,128)(2,1)S(1)}, u32[]{:S(2)}) copy-start(bf16[192,768]{1,0:T(8,128)(2,1)S(1)} %collective-permute-done.14.refs_1_) | copy-start | bytes 884740
  291.2 25.8 %collective-permute-start.19 = (bf16[192,768]{1,0:T(8,128)(2,1)S(1)}, bf16[192,768]{1,0:T(8,128)(2,1)S(1)}, u32[]{:S(2)}, u32[]{:S(2)}) collective-permute-start(bf16[192,768]{1,0:T(8,128)(2,1)S(1)} %copy-done.33), channel_id=1, source_target_pairs={{0,3},{1,2},{2,1},{3,0},{4,7},{5,6},{6,5},{7,4},{8,11},{9,10},{10,... | collective-permute-start | bytes 884744 | tf_op jit(solution)/shard_map/ppermute | solution.py:898
  298.9 18.0 %copy-start.18 = (bf16[192,768]{1,0:T(8,128)(2,1)}, bf16[192,768]{1,0:T(8,128)(2,1)S(1)}, u32[]{:S(2)}) copy-start(bf16[192,768]{1,0:T(8,128)(2,1)S(1)} %collective-permute-done.15.refs_2_) | copy-start | bytes 884740
  304.3 12.6 %copy-start.19 = (bf16[192,768]{1,0:T(8,128)(2,1)}, bf16[192,768]{1,0:T(8,128)(2,1)S(1)}, u32[]{:S(2)}) copy-start(bf16[192,768]{1,0:T(8,128)(2,1)S(1)} %collective-permute-done.16.refs_3_) | copy-start | bytes 884740
  304.3 12.6 %copy-start.20 = (bf16[192,768]{1,0:T(8,128)(2,1)}, bf16[192,768]{1,0:T(8,128)(2,1)S(1)}, u32[]{:S(2)}) copy-start(bf16[192,768]{1,0:T(8,128)(2,1)S(1)} %collective-permute-done.17.refs_5_) | copy-start | bytes 884740
  (12 other events, 21.7 us)
Sparse Core Ops, SparseCore 0:
  267.2 50.5 all-gather.6
  320.0 68.7 all-gather.4
